TPU v7x, 768 devices: a whole 4x8x12 slice. The times are simulated.
768 devices in a mesh: seq: 96 (over y, z), head: 8 (over x, core).
Axes of the slice: x: 4, y: 8, z: 12, core: 2. Of those that a mesh axis runs over, the one named last changes fastest.
Arguments:
- queries: bfloat16 [24576, 8192], P('seq', 'head'), may hold values from -125 to 125
- keys: bfloat16 [24576, 1024], P(('seq', 'head')), may hold values from -6 to 6
- values: bfloat16 [24576, 1024], P(('seq', 'head')), may hold values from -6 to 6
- header: int32 [192], P('seq'), may hold values from 0 to 191, as said below
- related: int32 [192, 3], P('seq'), may hold values from 0 to 191, as said below
- upstream: bfloat16 [24576, 8192], P('seq', 'head'), may hold values from -6 to 6
Outputs:
- attended: bfloat16 [24576, 8192], P('seq', 'head')
- query_grad: bfloat16 [24576, 8192], P('seq', 'head')
- key_grad: float32 [24576, 1024], P(('seq', 'head'))
- value_grad: float32 [24576, 1024], P(('seq', 'head'))
Inputs may be any that keep to these rules, and one draw needn't show every extreme that they name: Tables are runs of 1 to 8 consecutive row blocks, one of exactly 8, and the last row block is a table of its own; header[b] is the first block of the table that holds b. related[b, r] lies between header[b] and b.
All inputs are finite; a program needn't handle non-finite values.
Results may differ from a plain program's by a relative error of at most 0.04.
Values may be sent and summed in bfloat16 or wider, within the bound.
A program may use at most 32 MiB of HBM per device.

v0:
```python
import math

import jax
import jax.numpy as jnp
from jax import lax
from jax.sharding import PartitionSpec as P

BLOCK = 128
HEAD_DIM = 128
GROUP = 8
BLOCKS_DEV = 2
REACH = 4


def from_behind(block, axis, distance):
    devices = range(lax.axis_size(axis))
    route = [((i - distance) % len(devices), i) for i in devices]
    return lax.ppermute(block, axis, route)


def per_device(queries, keys, values, header, related, upstream):
    row_count = queries.shape[0]
    seq_count = lax.axis_size("seq")
    total_blocks = BLOCKS_DEV * seq_count
    score_scale = 1.0 / math.sqrt(HEAD_DIM)
    key_head, value_head = (
        lax.all_to_all(keys, "head", split_axis=1, concat_axis=0, tiled=True),
        lax.all_to_all(values, "head", split_axis=1, concat_axis=0, tiled=True),
    )
    paired = jnp.concatenate([key_head, value_head], axis=1)
    shifted = [from_behind(paired, "seq", REACH - shard_index) for shard_index in range(REACH)]
    window = jnp.concatenate(shifted + [paired], axis=0)
    width_blocks = (REACH + 1) * BLOCKS_DEV
    window = window.reshape(width_blocks, BLOCK, 2 * HEAD_DIM)
    first_block = lax.axis_index("seq") * BLOCKS_DEV
    own_blocks = first_block + jnp.arange(BLOCKS_DEV, dtype=jnp.int32)
    listed = jnp.concatenate(
        [own_blocks[:, None], ((own_blocks - 1) % total_blocks)[:, None], header[:, None], related],
        axis=1,
    )
    local_index = (listed - first_block + REACH * BLOCKS_DEV) % total_blocks
    chosen = jnp.take(window, local_index.reshape(-1), axis=0).reshape(
        BLOCKS_DEV, 6 * BLOCK, 2 * HEAD_DIM
    )
    grads = jnp.zeros((width_blocks, BLOCK, 2 * HEAD_DIM), jnp.float32)
    attended_parts = []
    query_parts = []
    for block_index in range(BLOCKS_DEV):
        query_blk = queries[block_index * BLOCK : (block_index + 1) * BLOCK].reshape(
            BLOCK, GROUP, HEAD_DIM
        )
        upstream_blk = upstream[block_index * BLOCK : (block_index + 1) * BLOCK].reshape(
            BLOCK, GROUP, HEAD_DIM
        )
        key_blk = chosen[block_index, :, :HEAD_DIM]
        value_blk = chosen[block_index, :, HEAD_DIM:]
        scores = (
            jnp.einsum("ijd,cd->jic", query_blk, key_blk, preferred_element_type=jnp.float32)
            * score_scale
        )
        top_score = jnp.max(scores, axis=-1, keepdims=True)
        weights_exp = jnp.exp(scores - top_score)
        probs = weights_exp / jnp.sum(weights_exp, axis=-1, keepdims=True)
        probs_low = probs.astype(jnp.bfloat16)
        attended = jnp.einsum(
            "jic,cd->ijd", probs_low, value_blk, preferred_element_type=jnp.float32
        ).astype(jnp.bfloat16)
        delta = jnp.einsum(
            "ijd,ijd->ji", upstream_blk.astype(jnp.float32), attended.astype(jnp.float32)
        )
        dprobs = jnp.einsum(
            "ijd,cd->jic", upstream_blk, value_blk, preferred_element_type=jnp.float32
        )
        dscores_low = (probs * (dprobs - delta[..., None])).astype(jnp.bfloat16)
        query_grad = (
            jnp.einsum("jic,cd->ijd", dscores_low, key_blk, preferred_element_type=jnp.float32)
            * score_scale
        ).astype(jnp.bfloat16)
        key_part = (
            jnp.einsum("jic,ijd->cd", dscores_low, query_blk, preferred_element_type=jnp.float32)
            * score_scale
        )
        value_part = jnp.einsum(
            "jic,ijd->cd", probs_low, upstream_blk, preferred_element_type=jnp.float32
        )
        both_parts = jnp.concatenate([key_part, value_part], axis=1).reshape(6, BLOCK, 2 * HEAD_DIM)
        grads = grads.at[local_index[block_index]].add(both_parts)
        attended_parts.append(attended.reshape(BLOCK, GROUP * HEAD_DIM))
        query_parts.append(query_grad.reshape(BLOCK, GROUP * HEAD_DIM))
    by_shard = grads.reshape(REACH + 1, row_count, 2 * HEAD_DIM)
    gathered_sum = by_shard[REACH]
    for offset in range(1, REACH + 1):
        gathered_sum = gathered_sum + from_behind(
            by_shard[REACH - offset].astype(jnp.bfloat16), "seq", -offset
        ).astype(jnp.float32)
    key_grad, value_grad = (
        lax.all_to_all(
            gathered_sum[:, :HEAD_DIM].astype(jnp.bfloat16),
            "head",
            split_axis=0,
            concat_axis=1,
            tiled=True,
        ).astype(jnp.float32),
        lax.all_to_all(
            gathered_sum[:, HEAD_DIM:].astype(jnp.bfloat16),
            "head",
            split_axis=0,
            concat_axis=1,
            tiled=True,
        ).astype(jnp.float32),
    )
    attended_all = jnp.concatenate(attended_parts, axis=0)
    query_all = jnp.concatenate(query_parts, axis=0)
    return (attended_all, query_all, key_grad, value_grad)


def solution(mesh):
    return jax.shard_map(
        per_device,
        mesh=mesh,
        in_specs=(
            P("seq", "head"),
            P(("seq", "head"), None),
            P(("seq", "head"), None),
            P("seq"),
            P("seq", None),
            P("seq", "head"),
        ),
        out_specs=(
            P("seq", "head"),
            P("seq", "head"),
            P(("seq", "head"), None),
            P(("seq", "head"), None),
        ),
        check_vma=False,
    )
```

profile of v0, /device:TPU:1, one launch (start us, length us, event | category | flops | bytes accessed | tf_op | source)
XLA Modules:
  0.0 147.4 jit_solution(9358069079915398886)
XLA Ops:
  0.7 0.8 copy-done
  1.5 0.6 copy_bitcast_fusion.3
  2.1 13.8 %all-to-all-start = ((bf16[32,8,128]{2,0,1:T(8,128)(2,1)}), bf16[32,8,128]{2,0,1:T(8,128)(2,1)S(1)}, u32[]{:S(2)}, u32[]{:S(2)}) async-start(bf16[32,8,128]{2,0,1:T(8,128)(2,1)} %copy_bitcast_fusion.3), calls=%async_computation | async-start | bytes 131072 | tf_op jit(solution)/shard_map/all_to_all | solution.py:27
  15.9 0.7 copy.89
  16.6 1.5 %copy_bitcast_fusion.2 = bf16[32,8,128]{2,0,1:T(8,128)(2,1)} fusion(bf16[32,1024]{1,0:T(8,128)(2,1)} %param.8), kind=kLoop, calls=%fused_computation.66 | loop fusion | bytes 131072 | tf_op jit(solution)/shard_map/all_to_all | solution.py:28
  18.1 1.1 fusion.46
  19.4 1.3 all-to-all-done
  20.8 4.0 %all-to-all-start.1 = ((bf16[32,8,128]{2,0,1:T(8,128)(2,1)}), bf16[32,8,128]{2,0,1:T(8,128)(2,1)S(1)}, u32[]{:S(2)}, u32[]{:S(2)}) async-start(bf16[32,8,128]{2,0,1:T(8,128)(2,1)} %copy_bitcast_fusion.2), calls=%async_computation.1 | async-start | bytes 131072 | tf_op jit(solution)/shard_map/all_to_all | solution.py:28
  24.9 4.8 %all-to-all-done.1 = bf16[32,8,128]{2,0,1:T(8,128)(2,1)S(1)} async-done(((bf16[32,8,128]{2,0,1:T(8,128)(2,1)}), bf16[32,8,128]{2,0,1:T(8,128)(2,1)S(1)}, u32[]{:S(2)}, u32[]{:S(2)}) %all-to-all-start.1) | async-done | bytes 65568 | tf_op jit(solution)/shard_map/all_to_all | solution.py:28
  29.7 2.6 %collective-permute-start = (bf16[256,256]{1,0:T(8,128)(2,1)S(1)}, bf16[256,256]{1,0:T(8,128)(2,1)S(1)}, u32[]{:S(2)}, u32[]{:S(2)}) collective-permute-start(bf16[256,256]{1,0:T(8,128)(2,1)S(1)} %pad_maximum_fusion.4), channel_id=1, source_target_pairs={{736,0},{744,8},{752,16},{760,24},{0,32},{8,40},{16,48},{24,56},{3... | collective-permute-start | bytes 393224 | tf_op jit(solution)/shard_map/ppermute | solution.py:18
  32.4 7.3 %collective-permute-start.1 = (bf16[256,256]{1,0:T(8,128)(2,1)S(1)}, bf16[256,256]{1,0:T(8,128)(2,1)S(1)}, u32[]{:S(2)}, u32[]{:S(2)}) collective-permute-start(bf16[256,256]{1,0:T(8,128)(2,1)S(1)} %pad_maximum_fusion.4), channel_id=1, source_target_pairs={{744,0},{752,8},{760,16},{0,24},{8,32},{16,40},{24,48},{32,56},{40... | collective-permute-start | bytes 393224 | tf_op jit(solution)/shard_map/ppermute | solution.py:18
  39.7 0.8 copy.154
  40.6 0.8 copy.155
  41.4 0.2 copy.156
  41.6 0.8 copy.157
  42.4 3.1 %collective-permute-start.3 = (bf16[256,256]{1,0:T(8,128)(2,1)S(1)}, bf16[256,256]{1,0:T(8,128)(2,1)S(1)}, u32[]{:S(2)}, u32[]{:S(2)}) collective-permute-start(bf16[256,256]{1,0:T(8,128)(2,1)S(1)} %pad_maximum_fusion.4), channel_id=1, source_target_pairs={{760,0},{0,8},{8,16},{16,24},{24,32},{32,40},{40,48},{48,56},{56,6... | collective-permute-start | bytes 393224 | tf_op jit(solution)/shard_map/ppermute | solution.py:18
  45.5 4.0 %collective-permute-start.2 = (bf16[256,256]{1,0:T(8,128)(2,1)S(1)}, bf16[256,256]{1,0:T(8,128)(2,1)S(1)}, u32[]{:S(2)}, u32[]{:S(2)}) collective-permute-start(bf16[256,256]{1,0:T(8,128)(2,1)S(1)} %pad_maximum_fusion.4), channel_id=1, source_target_pairs={{752,0},{760,8},{0,16},{8,24},{16,32},{24,40},{32,48},{40,56},{48,... | collective-permute-start | bytes 393224 | tf_op jit(solution)/shard_map/ppermute | solution.py:18
  49.6 7.6 %collective-permute-done.1 = bf16[256,256]{1,0:T(8,128)(2,1)S(1)} collective-permute-done((bf16[256,256]{1,0:T(8,128)(2,1)S(1)}, bf16[256,256]{1,0:T(8,128)(2,1)S(1)}, u32[]{:S(2)}, u32[]{:S(2)}) %collective-permute-start.1) | collective-permute-done | bytes 131104 | tf_op jit(solution)/shard_map/ppermute | solution.py:18
  57.1 10.2 %collective-permute-done.2 = bf16[256,256]{1,0:T(8,128)(2,1)S(1)} collective-permute-done((bf16[256,256]{1,0:T(8,128)(2,1)S(1)}, bf16[256,256]{1,0:T(8,128)(2,1)S(1)}, u32[]{:S(2)}, u32[]{:S(2)}) %collective-permute-start.2) | collective-permute-done | bytes 131104 | tf_op jit(solution)/shard_map/ppermute | solution.py:18
  67.4 0.6 gather_fusion
  68.0 1.2 bitcast_select_fusion
  69.2 2.2 %fusion.48 = (f32[8,128]{1,0:T(8,128)S(1)}, f32[8,128,768]{1,2,0:T(8,128)S(1)}) fusion(bf16[128,8,128]{0,2,1:T(8,128)(2,1)} %bitcast.219, bf16[2,768,256]{2,1,0:T(8,128)(2,1)} %bitcast_select_fusion), kind=kOutput, calls=%fused_computation.97 | convolution fusion | flops 203686656 | bytes 3608576 | tf_op jit(solution)/shard_map/sub | solution.py:62
  71.4 0.3 fusion.19
  71.7 0.8 copy-done.2
  72.6 1.1 fusion.24
  73.7 0.6 convolution_bitcast_fusion
  74.4 0.6 fusion.3
  75.0 0.3 copy-done.7
  75.3 0.6 fusion.22
  76.0 1.1 fusion.21
  77.2 1.2 copy.117
  78.3 2.2 %fusion.49 = (f32[8,128]{1,0:T(8,128)S(1)}, f32[8,128,768]{1,2,0:T(8,128)S(1)}) fusion(bf16[128,8,128]{0,2,1:T(8,128)(2,1)} %bitcast.216, bf16[2,768,256]{2,1,0:T(8,128)(2,1)} %bitcast_select_fusion), kind=kOutput, calls=%fused_computation.98 | convolution fusion | flops 203686656 | bytes 3608576 | tf_op jit(solution)/shard_map/sub | solution.py:62
  80.5 0.3 fusion.18
  80.8 1.4 copy-done.1
  82.2 1.1 fusion.25
  83.3 0.6 convolution_bitcast_fusion.2
  84.0 2.5 %fusion.5 = bf16[8,128,768]{1,2,0:T(8,128)(2,1)S(1)} fusion(bf16[128,8,128]{0,2,1:T(8,128)(2,1)S(1)} %bitcast.212, f32[8,128]{1,0:T(8,128)S(1)} %get-tuple-element.25, f32[8,128,768]{1,2,0:T(8,128)} %copy-done.1, f32[8,128]{1,0:T(8,128)S(1)} %get-tuple-element.21, bf16[2,768,256]{2,1,0:T(8,128)(2,1)S(1)} %copy-done.3), kind=kOutput, calls=%fused_computation.10 | convolution fusion | flops 204472320 | bytes 5185536 | tf_op jit(solution)/shard_map/ijd,cd->jic/dot_general | solution.py:71
  86.5 0.6 fusion.23
  87.2 1.2 copy.114
  88.4 0.1 broadcast_in_dim.35
  88.5 2.2 %scatter_fusion = f32[10,128,256]{2,1,0:T(8,128)S(1)} fusion(f32[10,128,256]{2,1,0:T(8,128)S(1)} %broadcast_in_dim.35, s32[6]{0:T(128)S(1)} %get-tuple-element.18, f32[6,128,256]{2,1,0:T(8,128)} %bitcast.209), kind=kCustom, calls=%fused_computation.1 | custom fusion | flops 196608 | bytes 2359320 | tf_op jit(solution)/shard_map/scatter-add | solution.py:87
  90.7 2.2 %scatter_fusion.1 = f32[10,128,256]{2,1,0:T(8,128)S(1)} fusion(f32[10,128,256]{2,1,0:T(8,128)S(1)} %scatter_fusion, s32[6]{0:T(128)S(1)} %get-tuple-element.17, f32[6,128,256]{2,1,0:T(8,128)} %bitcast.208), kind=kCustom, calls=%fused_computation.2 | custom fusion | flops 196608 | bytes 2359320 | tf_op jit(solution)/shard_map/scatter-add | solution.py:87
  93.0 0.8 fusion.44
  93.8 8.0 %collective-permute-start.7 = (bf16[256,256]{1,0:T(8,128)(2,1)}, bf16[256,256]{1,0:T(8,128)(2,1)}, u32[]{:S(2)}, u32[]{:S(2)}) collective-permute-start(bf16[256,256]{1,0:T(8,128)(2,1)} %bitcast.58), channel_id=1, source_target_pairs={{32,0},{40,8},{48,16},{56,24},{64,32},{72,40},{80,48},{88,56},{96,... | collective-permute-start | bytes 393224 | tf_op jit(solution)/shard_map/ppermute | solution.py:18
  101.8 1.9 %collective-permute-start.4 = (bf16[256,256]{1,0:T(8,128)(2,1)}, bf16[256,256]{1,0:T(8,128)(2,1)}, u32[]{:S(2)}, u32[]{:S(2)}) collective-permute-start(bf16[256,256]{1,0:T(8,128)(2,1)} %bitcast.55), channel_id=1, source_target_pairs={{8,0},{16,8},{24,16},{32,24},{40,32},{48,40},{56,48},{64,56},{72,6... | collective-permute-start | bytes 393224 | tf_op jit(solution)/shard_map/ppermute | solution.py:18
  103.7 2.2 %collective-permute-start.6 = (bf16[256,256]{1,0:T(8,128)(2,1)}, bf16[256,256]{1,0:T(8,128)(2,1)}, u32[]{:S(2)}, u32[]{:S(2)}) collective-permute-start(bf16[256,256]{1,0:T(8,128)(2,1)} %bitcast.57), channel_id=1, source_target_pairs={{24,0},{32,8},{40,16},{48,24},{56,32},{64,40},{72,48},{80,56},{88,... | collective-permute-start | bytes 393224 | tf_op jit(solution)/shard_map/ppermute | solution.py:18
  106.0 3.9 %collective-permute-start.5 = (bf16[256,256]{1,0:T(8,128)(2,1)}, bf16[256,256]{1,0:T(8,128)(2,1)}, u32[]{:S(2)}, u32[]{:S(2)}) collective-permute-start(bf16[256,256]{1,0:T(8,128)(2,1)} %bitcast.56), channel_id=1, source_target_pairs={{16,0},{24,8},{32,16},{40,24},{48,32},{56,40},{64,48},{72,56},{80,... | collective-permute-start | bytes 393224 | tf_op jit(solution)/shard_map/ppermute | solution.py:18
  109.9 2.0 %fusion.20 = bf16[128,8,128]{2,0,1:T(8,128)(2,1)} fusion(bf16[8,128,768]{1,2,0:T(8,128)(2,1)S(1)} %fusion.5, bf16[2,768,256]{2,1,0:T(8,128)(2,1)} %bitcast_select_fusion), kind=kOutput, calls=%fused_computation.29 | convolution fusion | flops 201588736 | bytes 2031616 | tf_op jit(solution)/shard_map/jic,cd->ijd/dot_general | solution.py:76
  112.0 0.1 copy.101
  112.1 1.1 copy.111
  113.2 0.1 copy.110
  113.4 0.1 copy.100
  113.5 0.8 pad_maximum_fusion.3
  114.4 9.9 %collective-permute-done.6 = bf16[256,256]{1,0:T(8,128)(2,1)} collective-permute-done((bf16[256,256]{1,0:T(8,128)(2,1)}, bf16[256,256]{1,0:T(8,128)(2,1)}, u32[]{:S(2)}, u32[]{:S(2)}) %collective-permute-start.6) | collective-permute-done | bytes 131104 | tf_op jit(solution)/shard_map/ppermute | solution.py:18
  124.2 2.2 %collective-permute-done.5 = bf16[256,256]{1,0:T(8,128)(2,1)} collective-permute-done((bf16[256,256]{1,0:T(8,128)(2,1)}, bf16[256,256]{1,0:T(8,128)(2,1)}, u32[]{:S(2)}, u32[]{:S(2)}) %collective-permute-start.5) | collective-permute-done | bytes 131104 | tf_op jit(solution)/shard_map/ppermute | solution.py:18
  126.4 1.2 fusion.33
  127.6 0.7 fusion.47
  128.3 4.7 %all-to-all-start.3 = ((bf16[8,32,128]{2,1,0:T(8,128)(2,1)}), bf16[8,32,128]{2,1,0:T(8,128)(2,1)S(1)}, u32[]{:S(2)}, u32[]{:S(2)}) async-start(bf16[8,32,128]{2,1,0:T(8,128)(2,1)} %bitcast.61), calls=%async_computation.3 | async-start | bytes 131072 | tf_op jit(solution)/shard_map/all_to_all | solution.py:104
  133.0 0.8 pad_maximum_fusion.2
  133.8 4.0 %all-to-all-done.3 = bf16[8,32,128]{2,1,0:T(8,128)(2,1)S(1)} async-done(((bf16[8,32,128]{2,1,0:T(8,128)(2,1)}), bf16[8,32,128]{2,1,0:T(8,128)(2,1)S(1)}, u32[]{:S(2)}, u32[]{:S(2)}) %all-to-all-start.3) | async-done | bytes 65568 | tf_op jit(solution)/shard_map/all_to_all | solution.py:104
  137.8 4.0 %all-to-all-start.2 = ((bf16[8,32,128]{2,1,0:T(8,128)(2,1)}), bf16[8,32,128]{2,1,0:T(8,128)(2,1)S(1)}, u32[]{:S(2)}, u32[]{:S(2)}) async-start(bf16[8,32,128]{2,1,0:T(8,128)(2,1)} %bitcast.59), calls=%async_computation.2 | async-start | bytes 131072 | tf_op jit(solution)/shard_map/all_to_all | solution.py:97
  141.9 0.7 copy_bitcast_fusion
  142.5 4.2 %all-to-all-done.2 = bf16[8,32,128]{2,1,0:T(8,128)(2,1)S(1)} async-done(((bf16[8,32,128]{2,1,0:T(8,128)(2,1)}), bf16[8,32,128]{2,1,0:T(8,128)(2,1)S(1)}, u32[]{:S(2)}, u32[]{:S(2)}) %all-to-all-start.2) | async-done | bytes 65568 | tf_op jit(solution)/shard_map/all_to_all | solution.py:97
  146.7 0.7 copy_bitcast_fusion.1
  (43 shorter events, 0.8 us)
Async XLA Ops:
  0.6 0.8 copy-start
  0.6 18.5 %copy-start.10 = (bf16[256,1024]{1,0:T(8,128)(2,1)S(1)}, bf16[256,1024]{1,0:T(8,128)(2,1)}, u32[]{:S(2)}) copy-start(bf16[256,1024]{1,0:T(8,128)(2,1)} %param.11) | copy-start | bytes 1572868
  1.5 17.8 %copy-start.11 = (s32[2,3]{1,0:T(2,128)S(1)}, s32[2,3]{1,0:T(2,128)}, u32[]{:S(2)}) copy-start(s32[2,3]{1,0:T(2,128)} %param.10) | copy-start | bytes 76
  2.1 18.6 %all-to-all-start = ((bf16[32,8,128]{2,0,1:T(8,128)(2,1)}), bf16[32,8,128]{2,0,1:T(8,128)(2,1)S(1)}, u32[]{:S(2)}, u32[]{:S(2)}) async-start(bf16[32,8,128]{2,0,1:T(8,128)(2,1)} %copy_bitcast_fusion.3), calls=%async_computation | async-start | bytes 131072 | tf_op jit(solution)/shard_map/all_to_all | solution.py:27
  20.8 8.9 %all-to-all-start.1 = ((bf16[32,8,128]{2,0,1:T(8,128)(2,1)}), bf16[32,8,128]{2,0,1:T(8,128)(2,1)S(1)}, u32[]{:S(2)}, u32[]{:S(2)}) async-start(bf16[32,8,128]{2,0,1:T(8,128)(2,1)} %copy_bitcast_fusion.2), calls=%async_computation.1 | async-start | bytes 131072 | tf_op jit(solution)/shard_map/all_to_all | solution.py:28
  29.7 19.9 %collective-permute-start = (bf16[256,256]{1,0:T(8,128)(2,1)S(1)}, bf16[256,256]{1,0:T(8,128)(2,1)S(1)}, u32[]{:S(2)}, u32[]{:S(2)}) collective-permute-start(bf16[256,256]{1,0:T(8,128)(2,1)S(1)} %pad_maximum_fusion.4), channel_id=1, source_target_pairs={{736,0},{744,8},{752,16},{760,24},{0,32},{8,40},{16,48},{24,56},{3... | collective-permute-start | bytes 393224 | tf_op jit(solution)/shard_map/ppermute | solution.py:18
  32.4 24.8 %collective-permute-start.1 = (bf16[256,256]{1,0:T(8,128)(2,1)S(1)}, bf16[256,256]{1,0:T(8,128)(2,1)S(1)}, u32[]{:S(2)}, u32[]{:S(2)}) collective-permute-start(bf16[256,256]{1,0:T(8,128)(2,1)S(1)} %pad_maximum_fusion.4), channel_id=1, source_target_pairs={{744,0},{752,8},{760,16},{0,24},{8,32},{16,40},{24,48},{32,56},{40... | collective-permute-start | bytes 393224 | tf_op jit(solution)/shard_map/ppermute | solution.py:18
  42.4 25.0 %collective-permute-start.3 = (bf16[256,256]{1,0:T(8,128)(2,1)S(1)}, bf16[256,256]{1,0:T(8,128)(2,1)S(1)}, u32[]{:S(2)}, u32[]{:S(2)}) collective-permute-start(bf16[256,256]{1,0:T(8,128)(2,1)S(1)} %pad_maximum_fusion.4), channel_id=1, source_target_pairs={{760,0},{0,8},{8,16},{16,24},{24,32},{32,40},{40,48},{48,56},{56,6... | collective-permute-start | bytes 393224 | tf_op jit(solution)/shard_map/ppermute | solution.py:18
  45.5 21.9 %collective-permute-start.2 = (bf16[256,256]{1,0:T(8,128)(2,1)S(1)}, bf16[256,256]{1,0:T(8,128)(2,1)S(1)}, u32[]{:S(2)}, u32[]{:S(2)}) collective-permute-start(bf16[256,256]{1,0:T(8,128)(2,1)S(1)} %pad_maximum_fusion.4), channel_id=1, source_target_pairs={{752,0},{760,8},{0,16},{8,24},{16,32},{24,40},{32,48},{40,56},{48,... | collective-permute-start | bytes 393224 | tf_op jit(solution)/shard_map/ppermute | solution.py:18
  71.4 1.1 copy-start.2
  71.4 1.2 copy-start.4
  74.4 1.0 copy-start.7
  80.5 1.6 %copy-start.1 = (f32[8,128,768]{1,2,0:T(8,128)}, f32[8,128,768]{1,2,0:T(8,128)S(1)}, u32[]{:S(2)}) copy-start(f32[8,128,768]{1,2,0:T(8,128)S(1)} %get-tuple-element.22) | copy-start | bytes 9437188
  80.5 1.7 %copy-start.3 = (bf16[2,768,256]{2,1,0:T(8,128)(2,1)S(1)}, bf16[2,768,256]{2,1,0:T(8,128)(2,1)}, u32[]{:S(2)}) copy-start(bf16[2,768,256]{2,1,0:T(8,128)(2,1)} %bitcast_select_fusion) | copy-start | bytes 2359300
  84.0 2.6 %copy-start.5 = (bf16[128,1024]{0,1:T(8,128)(2,1)S(1)}, bf16[128,1024]{0,1:T(8,128)(2,1)}, u32[]{:S(2)}) copy-start(bf16[128,1024]{0,1:T(8,128)(2,1)} %copy.154) | copy-start | bytes 786436
  93.0 19.0 %copy-start.6 = (bf16[128,8,128]{2,0,1:T(8,128)(2,1)S(1)}, bf16[128,8,128]{2,0,1:T(8,128)(2,1)}, u32[]{:S(2)}) copy-start(bf16[128,8,128]{2,0,1:T(8,128)(2,1)} %get-tuple-element.24) | copy-start | bytes 786436
  93.8 20.6 %collective-permute-start.7 = (bf16[256,256]{1,0:T(8,128)(2,1)}, bf16[256,256]{1,0:T(8,128)(2,1)}, u32[]{:S(2)}, u32[]{:S(2)}) collective-permute-start(bf16[256,256]{1,0:T(8,128)(2,1)} %bitcast.58), channel_id=1, source_target_pairs={{32,0},{40,8},{48,16},{56,24},{64,32},{72,40},{80,48},{88,56},{96,... | collective-permute-start | bytes 393224 | tf_op jit(solution)/shard_map/ppermute | solution.py:18
  101.8 12.6 %collective-permute-start.4 = (bf16[256,256]{1,0:T(8,128)(2,1)}, bf16[256,256]{1,0:T(8,128)(2,1)}, u32[]{:S(2)}, u32[]{:S(2)}) collective-permute-start(bf16[256,256]{1,0:T(8,128)(2,1)} %bitcast.55), channel_id=1, source_target_pairs={{8,0},{16,8},{24,16},{32,24},{40,32},{48,40},{56,48},{64,56},{72,6... | collective-permute-start | bytes 393224 | tf_op jit(solution)/shard_map/ppermute | solution.py:18
  103.7 20.5 %collective-permute-start.6 = (bf16[256,256]{1,0:T(8,128)(2,1)}, bf16[256,256]{1,0:T(8,128)(2,1)}, u32[]{:S(2)}, u32[]{:S(2)}) collective-permute-start(bf16[256,256]{1,0:T(8,128)(2,1)} %bitcast.57), channel_id=1, source_target_pairs={{24,0},{32,8},{40,16},{48,24},{56,32},{64,40},{72,48},{80,56},{88,... | collective-permute-start | bytes 393224 | tf_op jit(solution)/shard_map/ppermute | solution.py:18
  105.9 7.4 %copy-start.8 = (bf16[128,8,128]{2,0,1:T(8,128)(2,1)S(1)}, bf16[128,8,128]{2,0,1:T(8,128)(2,1)}, u32[]{:S(2)}) copy-start(bf16[128,8,128]{2,0,1:T(8,128)(2,1)} %get-tuple-element.26) | copy-start | bytes 786436
  106.0 20.5 %collective-permute-start.5 = (bf16[256,256]{1,0:T(8,128)(2,1)}, bf16[256,256]{1,0:T(8,128)(2,1)}, u32[]{:S(2)}, u32[]{:S(2)}) collective-permute-start(bf16[256,256]{1,0:T(8,128)(2,1)} %bitcast.56), channel_id=1, source_target_pairs={{16,0},{24,8},{32,16},{40,24},{48,32},{56,40},{64,48},{72,56},{80,... | collective-permute-start | bytes 393224 | tf_op jit(solution)/shard_map/ppermute | solution.py:18
  111.9 1.3 copy-start.9
  128.3 9.6 %all-to-all-start.3 = ((bf16[8,32,128]{2,1,0:T(8,128)(2,1)}), bf16[8,32,128]{2,1,0:T(8,128)(2,1)S(1)}, u32[]{:S(2)}, u32[]{:S(2)}) async-start(bf16[8,32,128]{2,1,0:T(8,128)(2,1)} %bitcast.61), calls=%async_computation.3 | async-start | bytes 131072 | tf_op jit(solution)/shard_map/all_to_all | solution.py:104
  137.8 8.9 %all-to-all-start.2 = ((bf16[8,32,128]{2,1,0:T(8,128)(2,1)}), bf16[8,32,128]{2,1,0:T(8,128)(2,1)S(1)}, u32[]{:S(2)}, u32[]{:S(2)}) async-start(bf16[8,32,128]{2,1,0:T(8,128)(2,1)} %bitcast.59), calls=%async_computation.2 | async-start | bytes 131072 | tf_op jit(solution)/shard_map/all_to_all | solution.py:97
where the time goes:
time: 148 us; the launch traced here: 147 us
  starting transfers between devices  59.7 us (40%)
  waiting for transfers between devices  44.2 us (30%)
  local copies, waits for them, and re-layouts  16.4 us (11%)
  matrix products  15.5 us (10%)
  other arithmetic  10.6 us (7%)
    ppermute x8, starting transfers between devices, from_behind(): return lax.ppermute(block, axis, route)  33.1 us
    ppermute x8, waiting for transfers between devices, from_behind(): return lax.ppermute(block, axis, route)  29.9 us
    all_to_all x1, starting transfers between devices, per_device(): lax.all_to_all(keys, 'head', split_axis=1, concat_axis=0, tiled=True)  13.8 us
    unnamed x34, local copies, waits for them, and re-layouts  6.34 us
    all_to_all x1, waiting for transfers between devices, per_device(): lax.all_to_all(values, 'head', split_axis=1, concat_axis=0, tiled=True)  4.78 us
    all_to_all x1, starting transfers between devices, per_device(): lax.all_to_all(gathered_sum[:, HEAD_DIM:].astype(jnp.bfloat16), 'head', s...  4.69 us
    sub x2, matrix products, per_device(): weights_exp = jnp.exp(scores - top_score)  4.38 us
    scatter-add x2, other arithmetic, per_device(): grads = grads.at[local_index[block_index]].add(both_parts)  4.36 us
  transfers between devices with their start and end apart: 12, of which 8 were waited for; matrix products, arithmetic and copies ran while one was open for 8% of the time, Pallas kernels for 0%

commit v1 on v0

v1 whole, which is shorter than its diff:
```python
import functools
import math

import jax
import jax.numpy as jnp
from jax import lax
from jax.experimental import pallas as pl
from jax.experimental.pallas import tpu as pltpu
from jax.sharding import PartitionSpec as P

BLOCK = 128
D = 128
GROUP = 8
QROWS = BLOCK * GROUP
SPAN = 8
NPOS = 9
REACH = 4
QT = 512
BIG = 1e30
SCALE = 1.0 / math.sqrt(D)
C2 = SCALE * math.log2(math.e)
LOG2 = [math.log2(n) if n else 0.0 for n in range(SPAN)]
NT = (((1,), (1,)), ((), ()))
NN = (((1,), (0,)), ((), ()))
F32 = jnp.float32
BF16 = jnp.bfloat16


def dot(a, b, dims=NN):
    return lax.dot_general(a, b, dims, preferred_element_type=F32)


def kernel(
    seq_n,
    head_n,
    header,
    related,
    q_hbm,
    u_hbm,
    k_hbm,
    v_hbm,
    att_hbm,
    dq_hbm,
    dk_hbm,
    dv_hbm,
    q_r,
    u_r,
    win,
    tr,
    pbuf,
    dpbuf,
    plow,
    dlow,
    stats,
    mhist,
    sbuf,
    rbuf,
    gbuf,
    backb,
    widen,
    final,
    att_v,
    dq_v,
    a_send,
    a_recv,
    f_send,
    f_recv,
    r_send,
    r_recv,
    b_send,
    b_recv,
    ld_sem,
    out_sem,
):
    seq = lax.axis_index("seq")
    me = lax.axis_index("head")
    nxt = lax.rem(seq + 1, seq_n)
    prv = lax.rem(seq + seq_n - 1, seq_n)
    part = (2 * BLOCK) // head_n
    half = head_n // 2
    own = (NPOS - 2) * BLOCK

    barrier = pltpu.get_barrier_semaphore()
    for off in range(1, head_n):
        pl.semaphore_signal(
            barrier, inc=1, device_id={"head": lax.rem(me + off, head_n)}
        )
    pl.semaphore_signal(barrier, inc=1, device_id={"seq": nxt})
    pl.semaphore_signal(barrier, inc=1, device_id={"seq": prv})

    def load(n):
        t, j = n // GROUP, n % GROUP
        rows, cols = pl.ds(t * BLOCK, BLOCK), pl.ds(j * D, D)
        at = pl.ds(n * BLOCK, BLOCK)
        return (
            pltpu.make_async_copy(q_hbm.at[rows, cols], q_r.at[at, :], ld_sem.at[0, n]),
            pltpu.make_async_copy(u_hbm.at[rows, cols], u_r.at[at, :], ld_sem.at[1, n]),
        )

    for n in range(2 * GROUP):
        for copy in load(n):
            copy.start()

    pl.semaphore_wait(barrier, head_n + 1)

    def mine(x, h):
        return pl.ds(own + h * part, part)

    sends = []
    for x, src in ((0, k_hbm), (1, v_hbm)):
        pltpu.make_async_copy(
            src.at[:, pl.ds(me * D, D)],
            win.at[x, pl.ds(own + me * part, part), :],
            a_recv.at[x, me],
        ).start()
        for off in range(1, head_n):
            peer = lax.rem(me + off, head_n)
            copy = pltpu.make_async_remote_copy(
                src_ref=src.at[:, pl.ds(peer * D, D)],
                dst_ref=win.at[x, pl.ds(own + me * part, part), :],
                send_sem=a_send.at[x, off],
                recv_sem=a_recv.at[x, me],
                device_id={"head": peer},
            )
            copy.start()
            sends.append(copy)

    def gathered(x, hi):
        for h in range(half * hi, half * hi + half):
            ref = win.at[x, pl.ds(own + h * part, part), :]
            pltpu.make_async_copy(ref, ref, a_recv.at[x, h]).wait()

    def forward(x, k, hi):
        at = (NPOS - 2 - 2 * k + hi) * BLOCK
        return pltpu.make_async_remote_copy(
            src_ref=win.at[x, pl.ds(at, BLOCK), :],
            dst_ref=win.at[x, pl.ds(at - 2 * BLOCK, BLOCK), :],
            send_sem=f_send.at[x, k, hi],
            recv_sem=f_recv.at[x, k, hi],
            device_id={"seq": nxt},
        )

    def pass_on(x, k, hi):
        if k == REACH - 1 and hi == 0:
            return
        copy = forward(x, k, hi)
        copy.start()
        sends.append(copy)

    def arrive(x, k, hi):
        forward(x, k - 1, hi).wait_recv()

    def relay(x, k):
        for hi in (1, 0):
            if k == REACH and hi == 0:
                continue
            if k == 0:
                gathered(x, hi)
            else:
                arrive(x, k, hi)
            if k < REACH:
                pass_on(x, k, hi)

    counts = []
    for t in range(2):
        block = 2 * seq + t
        gaps = [block - header[t]] + [block - related[t, r] for r in range(3)]
        row = []
        for d in range(SPAN):
            total = sum(
                (jnp.where(gap == d, 1.0, 0.0) for gap in gaps),
                1.0 if d < 2 else 0.0,
            )
            bias = jnp.where(total > 0.5, 0.0, -BIG)
            for n in range(2, SPAN):
                bias = jnp.where(total > n - 0.5, LOG2[n] / C2, bias)
            row.append(bias)
        counts.append(row)

    def pieces(k):
        if k == 0:
            return ((0, SPAN - 1, 1), (1, SPAN - 2, 2))
        if k == REACH:
            return ((0, 0, 1),)
        low = NPOS - 2 - 2 * k
        return ((0, low, 2), (1, low - 1, 2))

    def cols_of(n):
        return pl.ds(pl.multiple_of(n * QT, QT), QT)

    def scores(k):
        for t, row, blocks in pieces(k):
            keys = win.at[0, pl.ds((row + t) * BLOCK, blocks * BLOCK), :]
            bias = [counts[t][SPAN - 1 - row - b] for b in range(blocks)]

            def body(n, carry, t=t, row=row, blocks=blocks, keys=keys, bias=bias):
                cols = cols_of(n)
                q = q_r[pl.ds(pl.multiple_of(t * QROWS + n * QT, QT), QT), :]
                s = dot(keys[...], q, NT)
                tops = [
                    jnp.max(s[b * BLOCK : (b + 1) * BLOCK], axis=0, keepdims=True)
                    + jnp.minimum(bias[b], 0.0)
                    for b in range(blocks)
                ]
                top = functools.reduce(jnp.maximum, tops)
                if k > 0:
                    old = stats[t, 0:1, cols]
                    top = jnp.maximum(top, old)
                total = None
                for b in range(blocks):
                    shift = top - bias[b]
                    e = jnp.exp2((s[b * BLOCK : (b + 1) * BLOCK] - shift) * C2)
                    pbuf[t, pl.ds((row + b) * BLOCK, BLOCK), cols] = e
                    add = jnp.sum(e, axis=0, keepdims=True)
                    total = add if total is None else total + add
                if k > 0:
                    total = total + stats[t, 1:2, cols] * jnp.exp2((old - top) * C2)
                stats[t, 0:1, cols] = top
                stats[t, 1:2, cols] = total
                mhist[t, k : k + 1, cols] = top
                return carry

            lax.fori_loop(0, QROWS // QT, body, 0)

    def finish_sums():
        for t in range(2):
            inv = 1.0 / stats[t, 1:2, :]
            for k in range(REACH + 1 - t):
                mhist[t, k : k + 1, :] = (
                    jnp.exp2((mhist[t, k : k + 1, :] - stats[t, 0:1, :]) * C2) * inv
                )
            stats[t, 2:3, :] = jnp.zeros((1, QROWS), F32)

    def normalise(k):
        for t, row, blocks in pieces(k):
            rows = pl.ds(row * BLOCK, blocks * BLOCK)

            def body(n, carry, t=t, rows=rows):
                cols = cols_of(n)
                plow[t, rows, cols] = (
                    pbuf[t, rows, cols] * mhist[t, k : k + 1, cols]
                ).astype(BF16)
                return carry

            lax.fori_loop(0, QROWS // QT, body, 0)

    def dprobs(k):
        for t, row, blocks in pieces(k):
            rows = pl.ds(row * BLOCK, blocks * BLOCK)
            vals = win.at[1, pl.ds((row + t) * BLOCK, blocks * BLOCK), :]

            def body(n, carry, t=t, rows=rows, vals=vals):
                cols = cols_of(n)
                u = u_r[pl.ds(pl.multiple_of(t * QROWS + n * QT, QT), QT), :]
                dp = dot(vals[...], u, NT)
                dpbuf[t, rows, cols] = dp
                stats[t, 2:3, cols] += jnp.sum(
                    dp * plow[t, rows, cols].astype(F32), axis=0, keepdims=True
                )
                return carry

            lax.fori_loop(0, QROWS // QT, body, 0)

    def dscores(k):
        for t, row, blocks in pieces(k):
            rows = pl.ds(row * BLOCK, blocks * BLOCK)

            def body(n, carry, t=t, rows=rows):
                cols = cols_of(n)
                delta = stats[t, 2:3, cols]
                p = pbuf[t, rows, cols] * mhist[t, k : k + 1, cols]
                dlow[t, rows, cols] = (p * (dpbuf[t, rows, cols] - delta)).astype(BF16)
                return carry

            lax.fori_loop(0, QROWS // QT, body, 0)

    def terms(x, k):
        left, right, factor = (
            (dlow, q_r, SCALE),
            (plow, u_r, 1.0),
        )[x]
        found = {}
        for t, row, blocks in pieces(k):
            out = dot(
                left[t, pl.ds(row * BLOCK, blocks * BLOCK), :],
                right[pl.ds(t * QROWS, QROWS), :],
            )
            first = row + t - (NPOS - 2 - 2 * k)
            for b in range(blocks):
                hi = first + b
                term = out[b * BLOCK : (b + 1) * BLOCK]
                found[hi] = found[hi] + term if hi in found else term
        return {hi: term * factor for hi, term in found.items()}

    def backward(x, k, hi):
        return pltpu.make_async_remote_copy(
            src_ref=sbuf.at[x, k - 1, hi],
            dst_ref=rbuf.at[x, k - 1, hi],
            send_sem=r_send.at[x, k - 1, hi],
            recv_sem=r_recv.at[x, k - 1, hi],
            device_id={"seq": prv},
        )

    def local_terms(x, k):
        for hi, term in terms(x, k).items():
            widen[x, k, hi] = term

    def reduce_send(x, k):
        for hi in (1, 0):
            if k == REACH and hi == 0:
                continue
            total = widen[x, k, hi]
            if k < REACH - 1 or (k == REACH - 1 and hi == 1):
                backward(x, k + 1, hi).wait_recv()
                total = total + rbuf[x, k, hi].astype(F32)
            if k > 0:
                sbuf[x, k - 1, hi] = total.astype(BF16)
                copy = backward(x, k, hi)
                copy.start()
                sends.append(copy)
            else:
                gbuf[x, pl.ds(hi * BLOCK, BLOCK), :] = total.astype(BF16)

    def return_home(x):
        pltpu.make_async_copy(
            gbuf.at[x, pl.ds(me * part, part), :],
            backb.at[x, me],
            b_recv.at[x, me],
        ).start()
        for off in range(1, head_n):
            peer = lax.rem(me + off, head_n)
            copy = pltpu.make_async_remote_copy(
                src_ref=gbuf.at[x, pl.ds(peer * part, part), :],
                dst_ref=backb.at[x, me],
                send_sem=b_send.at[x, off],
                recv_sem=b_recv.at[x, me],
                device_id={"head": peer},
            )
            copy.start()
            sends.append(copy)

    outs = []

    def write_home(x, target):
        for h in range(head_n):
            ref = backb.at[x, h]
            pltpu.make_async_copy(ref, ref, b_recv.at[x, h]).wait()
            final[x, :, h * D : (h + 1) * D] = backb[x, h].astype(F32)
        copy = pltpu.make_async_copy(final.at[x], target, out_sem.at[x])
        copy.start()
        outs.append(copy)

    def transposes(x):
        for p in range(NPOS):
            at = pl.ds(p * BLOCK, BLOCK)
            tr[x, :, at] = win[x, at, :].T

    def row_output(x, left, stage, target, factor, slot):
        for t in range(2):

            def body(n, carry, t=t):
                cols = pl.ds(pl.multiple_of(n * 2 * D, 2 * D), 2 * D)
                out = dot(tr[x, :, pl.ds(t * BLOCK, SPAN * BLOCK)], left[t, :, cols])
                for s in range(2):
                    part_cols = pl.ds(pl.multiple_of((2 * n + s) * D, D), D)
                    stage[pl.ds(t * BLOCK, BLOCK), part_cols] = (
                        out[:, s * D : (s + 1) * D].T * factor
                    ).astype(BF16)
                return carry

            lax.fori_loop(0, GROUP // 2, body, 0)
        copy = pltpu.make_async_copy(stage, target, out_sem.at[slot])
        copy.start()
        outs.append(copy)

    relay(0, 0)
    for n in range(2 * GROUP):
        for copy in load(n):
            copy.wait()
    relay(1, 0)
    scores(0)
    for k in range(1, REACH):
        relay(0, k)
        relay(1, k)
        scores(k)
    relay(0, REACH)
    scores(REACH)
    finish_sums()
    normalise(REACH)
    local_terms(1, REACH)
    reduce_send(1, REACH)
    normalise(3)
    local_terms(1, 3)
    normalise(2)
    local_terms(1, 2)
    normalise(1)
    local_terms(1, 1)
    reduce_send(1, 3)
    normalise(0)
    local_terms(1, 0)
    dprobs(0)
    dprobs(1)
    reduce_send(1, 2)
    dprobs(2)
    dprobs(3)
    relay(1, REACH)
    dprobs(REACH)
    dscores(REACH)
    local_terms(0, REACH)
    reduce_send(0, REACH)
    reduce_send(1, 1)
    dscores(3)
    local_terms(0, 3)
    reduce_send(0, 3)
    dscores(2)
    local_terms(0, 2)
    reduce_send(1, 0)
    return_home(1)
    reduce_send(0, 2)
    dscores(1)
    local_terms(0, 1)
    reduce_send(0, 1)
    dscores(0)
    local_terms(0, 0)
    transposes(1)
    row_output(1, plow, att_v, att_hbm, 1.0, 2)
    reduce_send(0, 0)
    return_home(0)
    transposes(0)
    row_output(0, dlow, dq_v, dq_hbm, SCALE, 3)
    write_home(1, dv_hbm)
    write_home(0, dk_hbm)
    for copy in sends:
        copy.wait_send()
    for copy in outs:
        copy.wait()


def per_device(queries, keys, values, header, related, upstream):
    seq_n, head_n = lax.axis_size("seq"), lax.axis_size("head")
    part = keys.shape[0]
    any_space = pl.BlockSpec(memory_space=pl.ANY)
    scalars = pl.BlockSpec(memory_space=pltpu.SMEM)
    dma = pltpu.SemaphoreType.DMA
    return pl.pallas_call(
        functools.partial(kernel, seq_n, head_n),
        out_shape=(
            jax.ShapeDtypeStruct(queries.shape, BF16),
            jax.ShapeDtypeStruct(queries.shape, BF16),
            jax.ShapeDtypeStruct(keys.shape, F32),
            jax.ShapeDtypeStruct(values.shape, F32),
        ),
        in_specs=[scalars, scalars] + [any_space] * 4,
        out_specs=(any_space,) * 4,
        scratch_shapes=[
            pltpu.VMEM((2 * QROWS, D), BF16),
            pltpu.VMEM((2 * QROWS, D), BF16),
            pltpu.VMEM((2, NPOS * BLOCK, D), BF16),
            pltpu.VMEM((2, D, NPOS * BLOCK), BF16),
            pltpu.VMEM((2, SPAN * BLOCK, QROWS), F32),
            pltpu.VMEM((2, SPAN * BLOCK, QROWS), F32),
            pltpu.VMEM((2, SPAN * BLOCK, QROWS), BF16),
            pltpu.VMEM((2, SPAN * BLOCK, QROWS), BF16),
            pltpu.VMEM((2, 8, QROWS), F32),
            pltpu.VMEM((2, 8, QROWS), F32),
            pltpu.VMEM((2, REACH, 2, BLOCK, D), BF16),
            pltpu.VMEM((2, REACH, 2, BLOCK, D), BF16),
            pltpu.VMEM((2, 2 * BLOCK, D), BF16),
            pltpu.VMEM((2, head_n, part, D), BF16),
            pltpu.VMEM((2, REACH + 1, 2, BLOCK, D), F32),
            pltpu.VMEM((2, part, head_n * D), F32),
            pltpu.VMEM((2 * BLOCK, GROUP * D), BF16),
            pltpu.VMEM((2 * BLOCK, GROUP * D), BF16),
            dma((2, head_n)),
            dma((2, head_n)),
            dma((2, REACH, 2)),
            dma((2, REACH, 2)),
            dma((2, REACH, 2)),
            dma((2, REACH, 2)),
            dma((2, head_n)),
            dma((2, head_n)),
            dma((2, 2 * GROUP)),
            dma((4,)),
        ],
        compiler_params=pltpu.CompilerParams(
            collective_id=0,
            has_side_effects=True,
            vmem_limit_bytes=60 * 1024 * 1024,
        ),
        name="table_attention",
    )(header, related, queries, upstream, keys, values)


def solution(mesh):
    return jax.shard_map(
        per_device,
        mesh=mesh,
        in_specs=(
            P("seq", "head"),
            P(("seq", "head"), None),
            P(("seq", "head"), None),
            P("seq"),
            P("seq", None),
            P("seq", "head"),
        ),
        out_specs=(
            P("seq", "head"),
            P("seq", "head"),
            P(("seq", "head"), None),
            P(("seq", "head"), None),
        ),
        check_vma=False,
    )
```

time: 148 us -> 68.5 us (0.46)
  Pallas kernels: 0 us -> 63.1 us
  starting transfers between devices: 59.7 us -> 0 us
  waiting for transfers between devices: 44.2 us -> 0 us
  matrix products: 15.5 us -> 0 us
  local copies, waits for them, and re-layouts: 16.4 us -> 4.56 us
  other arithmetic: 10.6 us -> 0 us
    pallas_call x0 -> x1, Pallas kernels: none -> 63.1 us  [per_device(): pl.pallas_call(functools.partial(kernel, seq_n, head_n), out_shape=(jax.S...]
    ppermute x8 -> x0, starting transfers between devices: 33.1 us -> none  [from_behind(): return lax.ppermute(block, axis, route)]
    ppermute x8 -> x0, waiting for transfers between devices: 29.9 us -> none  [from_behind(): return lax.ppermute(block, axis, route)]
    all_to_all x4 -> x0, starting transfers between devices: 26.5 us -> none  [the longest x1 13.8 us: per_device(): lax.all_to_all(keys, 'head', split_axis=1, concat_axis=0, tiled=True)]
    all_to_all x4 -> x0, waiting for transfers between devices: 14.4 us -> none  [the longest x1 4.78 us: per_device(): lax.all_to_all(values, 'head', split_axis=1, concat_axis=0, tiled=True)]
    dot_general x10 -> x0, matrix products: 11.1 us -> none  [the longest x2 3.17 us: per_device(): jnp.einsum('jic,cd->ijd', dscores_low, key_blk, preferred_element_type=jn...]
    sub x2 -> x0, matrix products: 4.38 us -> none  [per_device(): weights_exp = jnp.exp(scores - top_score)]
    scatter-add x2 -> x0, other arithmetic: 4.36 us -> none  [per_device(): grads = grads.at[local_index[block_index]].add(both_parts)]
  transfers between devices with their start and end apart: 12 -> 0, of which waited for: 8 -> 0; matrix products, arithmetic and copies ran while one was open for 8% -> 0% of each run, Pallas kernels for 0% -> 0%
where the time goes in v1:
time: 68.5 us; the launch traced here: 68.3 us
  Pallas kernels  63.1 us (92%)
  local copies, waits for them, and re-layouts  4.56 us (7%)
    pallas_call x1, Pallas kernels, per_device(): pl.pallas_call(functools.partial(kernel, seq_n, head_n), out_shape=(jax.S...  63.1 us
    unnamed x10, local copies, waits for them, and re-layouts  4.56 us

profile of v1, /device:TPU:1, one launch (start us, length us, event | category | flops | bytes accessed | tf_op | source)
XLA Modules:
  0.0 68.3 jit_solution(833435472682556329)
XLA Ops:
  0.6 63.1 %table_attention.1 = (bf16[256,1024]{1,0:T(8,128)(2,1)}, bf16[256,1024]{1,0:T(8,128)(2,1)}, f32[32,1024]{1,0:T(8,128)}, f32[32,1024]{1,0:T(8,128)}) custom-call(s32[2]{0:T(128)} %header.1, s32[2,3]{1,0:T(2,128)} %related.1, bf16[256,1024]{1,0:T(8,128)(2,1)} %q_hbm.1, bf16[256,1024]{1,0:T(8,128)(2,1)} %u_hbm.1, bf16[32,1024]{1,0:T(8,128)(2,1)} %k_hbm.1, ...), custom_call_target="tpu_custom_call" | custom-call | tf_op jit(solution)/shard_map/table_attention/pallas_call | solution.py:445
  63.7 0.0 copy-start
  63.7 1.9 %copy.14 = bf16[256,1024]{1,0:T(8,128)(2,1)} copy(bf16[256,1024]{1,0:T(8,128)(2,1)} %get-tuple-element.8) | data formatting | bytes 1048576
  65.6 0.0 copy-done
  65.6 0.0 copy-start.2
  65.6 0.8 %copy.15 = bf16[256,1024]{1,0:T(8,128)(2,1)} copy(bf16[256,1024]{1,0:T(8,128)(2,1)S(1)} %copy-done) | data formatting | bytes 1048576
  66.4 0.2 copy-done.2
  66.7 0.0 copy-start.1
  66.7 0.7 copy.16
  67.3 0.3 copy-done.1
  67.6 0.7 copy.17
Async XLA Ops:
  63.7 1.9 %copy-start = (bf16[256,1024]{1,0:T(8,128)(2,1)S(1)}, bf16[256,1024]{1,0:T(8,128)(2,1)}, u32[]{:S(2)}) copy-start(bf16[256,1024]{1,0:T(8,128)(2,1)} %get-tuple-element.9) | copy-start | bytes 1572868
  65.6 1.0 %copy-start.2 = (f32[32,1024]{1,0:T(8,128)S(1)}, f32[32,1024]{1,0:T(8,128)}, u32[]{:S(2)}) copy-start(f32[32,1024]{1,0:T(8,128)} %get-tuple-element.10) | copy-start | bytes 393220
  66.7 1.0 %copy-start.1 = (f32[32,1024]{1,0:T(8,128)S(1)}, f32[32,1024]{1,0:T(8,128)}, u32[]{:S(2)}) copy-start(f32[32,1024]{1,0:T(8,128)} %get-tuple-element.11) | copy-start | bytes 393220

commit v2 on v1

--- a/solution.py
+++ b/solution.py
@@ -33,16 +33,15 @@
 def kernel(
     seq_n,
     head_n,
-    header,
-    related,
+    header_hbm,
+    related_hbm,
     q_hbm,
     u_hbm,
     k_hbm,
     v_hbm,
-    att_hbm,
-    dq_hbm,
-    dk_hbm,
-    dv_hbm,
+    home,
+    att_v,
+    dq_v,
     q_r,
     u_r,
     win,
@@ -53,14 +52,12 @@
     dlow,
     stats,
     mhist,
+    dsum,
     sbuf,
     rbuf,
     gbuf,
     backb,
     widen,
-    final,
-    att_v,
-    dq_v,
     a_send,
     a_recv,
     f_send,
@@ -70,7 +67,9 @@
     b_send,
     b_recv,
     ld_sem,
-    out_sem,
+    header,
+    related,
+    table_sem,
 ):
     seq = lax.axis_index("seq")
     me = lax.axis_index("head")
@@ -96,10 +95,6 @@
             pltpu.make_async_copy(q_hbm.at[rows, cols], q_r.at[at, :], ld_sem.at[0, n]),
             pltpu.make_async_copy(u_hbm.at[rows, cols], u_r.at[at, :], ld_sem.at[1, n]),
         )
-
-    for n in range(2 * GROUP):
-        for copy in load(n):
-            copy.start()
 
     pl.semaphore_wait(barrier, head_n + 1)
 
@@ -125,6 +120,16 @@
             copy.start()
             sends.append(copy)
 
+    tables = (
+        pltpu.make_async_copy(header_hbm, header, table_sem.at[0]),
+        pltpu.make_async_copy(related_hbm, related, table_sem.at[1]),
+    )
+    for copy in tables:
+        copy.start()
+    for n in range(2 * GROUP):
+        for copy in load(n):
+            copy.start()
+
     def gathered(x, hi):
         for h in range(half * hi, half * hi + half):
             ref = win.at[x, pl.ds(own + h * part, part), :]
@@ -160,22 +165,6 @@
                 arrive(x, k, hi)
             if k < REACH:
                 pass_on(x, k, hi)
-
-    counts = []
-    for t in range(2):
-        block = 2 * seq + t
-        gaps = [block - header[t]] + [block - related[t, r] for r in range(3)]
-        row = []
-        for d in range(SPAN):
-            total = sum(
-                (jnp.where(gap == d, 1.0, 0.0) for gap in gaps),
-                1.0 if d < 2 else 0.0,
-            )
-            bias = jnp.where(total > 0.5, 0.0, -BIG)
-            for n in range(2, SPAN):
-                bias = jnp.where(total > n - 0.5, LOG2[n] / C2, bias)
-            row.append(bias)
-        counts.append(row)
 
     def pieces(k):
         if k == 0:
@@ -229,20 +218,6 @@
                 mhist[t, k : k + 1, :] = (
                     jnp.exp2((mhist[t, k : k + 1, :] - stats[t, 0:1, :]) * C2) * inv
                 )
-            stats[t, 2:3, :] = jnp.zeros((1, QROWS), F32)
-
-    def normalise(k):
-        for t, row, blocks in pieces(k):
-            rows = pl.ds(row * BLOCK, blocks * BLOCK)
-
-            def body(n, carry, t=t, rows=rows):
-                cols = cols_of(n)
-                plow[t, rows, cols] = (
-                    pbuf[t, rows, cols] * mhist[t, k : k + 1, cols]
-                ).astype(BF16)
-                return carry
-
-            lax.fori_loop(0, QROWS // QT, body, 0)
 
     def dprobs(k):
         for t, row, blocks in pieces(k):
@@ -254,22 +229,34 @@
                 u = u_r[pl.ds(pl.multiple_of(t * QROWS + n * QT, QT), QT), :]
                 dp = dot(vals[...], u, NT)
                 dpbuf[t, rows, cols] = dp
-                stats[t, 2:3, cols] += jnp.sum(
-                    dp * plow[t, rows, cols].astype(F32), axis=0, keepdims=True
+                dsum[t, k : k + 1, cols] = jnp.sum(
+                    dp * pbuf[t, rows, cols], axis=0, keepdims=True
                 )
                 return carry
 
             lax.fori_loop(0, QROWS // QT, body, 0)
 
-    def dscores(k):
+    def finish_delta():
+        for t in range(2):
+            stats[t, 2:3, :] = sum(
+                mhist[t, k : k + 1, :] * dsum[t, k : k + 1, :]
+                for k in range(REACH + 1 - t)
+            )
+
+    def settle(k, probs=True, grads=True):
         for t, row, blocks in pieces(k):
             rows = pl.ds(row * BLOCK, blocks * BLOCK)
 
             def body(n, carry, t=t, rows=rows):
                 cols = cols_of(n)
-                delta = stats[t, 2:3, cols]
                 p = pbuf[t, rows, cols] * mhist[t, k : k + 1, cols]
-                dlow[t, rows, cols] = (p * (dpbuf[t, rows, cols] - delta)).astype(BF16)
+                if probs:
+                    plow[t, rows, cols] = p.astype(BF16)
+                if grads:
+                    delta = stats[t, 2:3, cols]
+                    dlow[t, rows, cols] = (
+                        p * (dpbuf[t, rows, cols] - delta)
+                    ).astype(BF16)
                 return carry
 
             lax.fori_loop(0, QROWS // QT, body, 0)
@@ -339,23 +326,18 @@
             copy.start()
             sends.append(copy)
 
-    outs = []
-
-    def write_home(x, target):
+    def write_home(x):
         for h in range(head_n):
             ref = backb.at[x, h]
             pltpu.make_async_copy(ref, ref, b_recv.at[x, h]).wait()
-            final[x, :, h * D : (h + 1) * D] = backb[x, h].astype(F32)
-        copy = pltpu.make_async_copy(final.at[x], target, out_sem.at[x])
-        copy.start()
-        outs.append(copy)
+        home[x] = backb[x]
 
     def transposes(x):
         for p in range(NPOS):
             at = pl.ds(p * BLOCK, BLOCK)
             tr[x, :, at] = win[x, at, :].T
 
-    def row_output(x, left, stage, target, factor, slot):
+    def row_output(x, left, stage, factor):
         for t in range(2):
 
             def body(n, carry, t=t):
@@ -369,89 +351,116 @@
                 return carry
 
             lax.fori_loop(0, GROUP // 2, body, 0)
-        copy = pltpu.make_async_copy(stage, target, out_sem.at[slot])
-        copy.start()
-        outs.append(copy)
-
     relay(0, 0)
+    for copy in tables:
+        copy.wait()
+    counts = []
+    for t in range(2):
+        block = 2 * seq + t
+        gaps = [block - header[t]] + [block - related[t, r] for r in range(3)]
+        row = []
+        for d in range(SPAN):
+            total = sum(
+                (jnp.where(gap == d, 1.0, 0.0) for gap in gaps),
+                1.0 if d < 2 else 0.0,
+            )
+            bias = jnp.where(total > 0.5, 0.0, -BIG)
+            for n in range(2, SPAN):
+                bias = jnp.where(total > n - 0.5, LOG2[n] / C2, bias)
+            row.append(bias)
+        counts.append(row)
+
     for n in range(2 * GROUP):
         for copy in load(n):
             copy.wait()
     relay(1, 0)
     scores(0)
+    dprobs(0)
     for k in range(1, REACH):
         relay(0, k)
+        scores(k)
         relay(1, k)
-        scores(k)
+        dprobs(k)
     relay(0, REACH)
     scores(REACH)
     finish_sums()
-    normalise(REACH)
+    settle(REACH, grads=False)
     local_terms(1, REACH)
     reduce_send(1, REACH)
-    normalise(3)
-    local_terms(1, 3)
-    normalise(2)
-    local_terms(1, 2)
-    normalise(1)
-    local_terms(1, 1)
-    reduce_send(1, 3)
-    normalise(0)
-    local_terms(1, 0)
-    dprobs(0)
-    dprobs(1)
-    reduce_send(1, 2)
-    dprobs(2)
-    dprobs(3)
     relay(1, REACH)
     dprobs(REACH)
-    dscores(REACH)
+    finish_delta()
+    settle(REACH, probs=False)
     local_terms(0, REACH)
     reduce_send(0, REACH)
+    settle(3)
+    local_terms(1, 3)
+    local_terms(0, 3)
+    settle(2)
+    reduce_send(1, 3)
+    reduce_send(0, 3)
+    local_terms(1, 2)
+    local_terms(0, 2)
+    settle(1)
+    local_terms(1, 1)
+    reduce_send(1, 2)
+    reduce_send(0, 2)
+    local_terms(0, 1)
+    settle(0)
+    local_terms(1, 0)
+    local_terms(0, 0)
     reduce_send(1, 1)
-    dscores(3)
-    local_terms(0, 3)
-    reduce_send(0, 3)
-    dscores(2)
-    local_terms(0, 2)
+    reduce_send(0, 1)
+    transposes(1)
+    row_output(1, plow, att_v, 1.0)
+    transposes(0)
     reduce_send(1, 0)
     return_home(1)
-    reduce_send(0, 2)
-    dscores(1)
-    local_terms(0, 1)
-    reduce_send(0, 1)
-    dscores(0)
-    local_terms(0, 0)
-    transposes(1)
-    row_output(1, plow, att_v, att_hbm, 1.0, 2)
     reduce_send(0, 0)
     return_home(0)
-    transposes(0)
-    row_output(0, dlow, dq_v, dq_hbm, SCALE, 3)
-    write_home(1, dv_hbm)
-    write_home(0, dk_hbm)
+    row_output(0, dlow, dq_v, SCALE)
+    write_home(1)
+    write_home(0)
     for copy in sends:
         copy.wait_send()
-    for copy in outs:
+
+
+def emit(home, att_v, dq_v, att, dq, dk, dv, wide, sems):
+    copies = [
+        pltpu.make_async_copy(att_v, att, sems.at[2]),
+        pltpu.make_async_copy(dq_v, dq, sems.at[3]),
+    ]
+    for copy in copies:
+        copy.start()
+    for x, target in ((0, dk), (1, dv)):
+        for h in range(home.shape[1]):
+            wide[x, :, h * D : (h + 1) * D] = home[x, h].astype(F32)
+        copy = pltpu.make_async_copy(wide.at[x], target, sems.at[x])
+        copy.start()
+        copies.append(copy)
+    for copy in copies:
         copy.wait()
 
 
 def per_device(queries, keys, values, header, related, upstream):
     seq_n, head_n = lax.axis_size("seq"), lax.axis_size("head")
     part = keys.shape[0]
-    any_space = pl.BlockSpec(memory_space=pl.ANY)
-    scalars = pl.BlockSpec(memory_space=pltpu.SMEM)
+    hbm = pl.BlockSpec(memory_space=pltpu.HBM)
     dma = pltpu.SemaphoreType.DMA
-    return pl.pallas_call(
+    vmem = pl.BlockSpec(memory_space=pltpu.VMEM)
+    inputs = [
+        pltpu.with_memory_space_constraint(x, pltpu.HBM)
+        for x in (header, related, queries, upstream, keys, values)
+    ]
+    home, att, dq = pl.pallas_call(
         functools.partial(kernel, seq_n, head_n),
         out_shape=(
+            jax.ShapeDtypeStruct((2, head_n, part, D), BF16),
             jax.ShapeDtypeStruct(queries.shape, BF16),
             jax.ShapeDtypeStruct(queries.shape, BF16),
-            jax.ShapeDtypeStruct(keys.shape, F32),
-            jax.ShapeDtypeStruct(values.shape, F32),
         ),
-        in_specs=[scalars, scalars] + [any_space] * 4,
-        out_specs=(any_space,) * 4,
+        in_specs=[hbm] * 6,
+        out_specs=(vmem,) * 3,
         scratch_shapes=[
             pltpu.VMEM((2 * QROWS, D), BF16),
             pltpu.VMEM((2 * QROWS, D), BF16),
@@ -463,14 +472,12 @@
             pltpu.VMEM((2, SPAN * BLOCK, QROWS), BF16),
             pltpu.VMEM((2, 8, QROWS), F32),
             pltpu.VMEM((2, 8, QROWS), F32),
+            pltpu.VMEM((2, 8, QROWS), F32),
             pltpu.VMEM((2, REACH, 2, BLOCK, D), BF16),
             pltpu.VMEM((2, REACH, 2, BLOCK, D), BF16),
             pltpu.VMEM((2, 2 * BLOCK, D), BF16),
             pltpu.VMEM((2, head_n, part, D), BF16),
             pltpu.VMEM((2, REACH + 1, 2, BLOCK, D), F32),
-            pltpu.VMEM((2, part, head_n * D), F32),
-            pltpu.VMEM((2 * BLOCK, GROUP * D), BF16),
-            pltpu.VMEM((2 * BLOCK, GROUP * D), BF16),
             dma((2, head_n)),
             dma((2, head_n)),
             dma((2, REACH, 2)),
@@ -480,15 +487,31 @@
             dma((2, head_n)),
             dma((2, head_n)),
             dma((2, 2 * GROUP)),
-            dma((4,)),
+            pltpu.SMEM(header.shape, jnp.int32),
+            pltpu.SMEM(related.shape, jnp.int32),
+            dma((2,)),
         ],
         compiler_params=pltpu.CompilerParams(
             collective_id=0,
             has_side_effects=True,
-            vmem_limit_bytes=60 * 1024 * 1024,
+            vmem_limit_bytes=44 * 1024 * 1024,
         ),
         name="table_attention",
-    )(header, related, queries, upstream, keys, values)
+    )(*inputs)
+    return pl.pallas_call(
+        emit,
+        out_shape=(
+            jax.ShapeDtypeStruct(queries.shape, BF16),
+            jax.ShapeDtypeStruct(queries.shape, BF16),
+            jax.ShapeDtypeStruct(keys.shape, F32),
+            jax.ShapeDtypeStruct(values.shape, F32),
+        ),
+        in_specs=[vmem] * 3,
+        out_specs=(hbm,) * 4,
+        scratch_shapes=[pltpu.VMEM((2,) + keys.shape, F32), dma((4,))],
+        compiler_params=pltpu.CompilerParams(vmem_limit_bytes=4 * 1024 * 1024),
+        name="write_results",
+    )(home, att, dq)
 
 
 def solution(mesh):

time: 68.5 us -> 58.3 us (0.85)
  Pallas kernels: 63.1 us -> 57.4 us
  local copies, waits for them, and re-layouts: 4.56 us -> 0 us
    pallas_call x1, Pallas kernels: 63.1 us -> 56.4 us  [per_device(): pl.pallas_call(functools.partial(kernel, seq_n, head_n), out_shape=(jax.S...]
    unnamed x10 -> x0, local copies, waits for them, and re-layouts: 4.56 us -> none
    pallas_call x0 -> x1, Pallas kernels: none -> 1.08 us  [per_device(): pl.pallas_call(emit, out_shape=(jax.ShapeDtypeStruct(queries.shape, BF16)...]
where the time goes in v2:
time: 58.3 us; the launch traced here: 58.1 us
  Pallas kernels  57.4 us (98%)
  between operations  0.64 us (1%)
    pallas_call x1, Pallas kernels, per_device(): pl.pallas_call(functools.partial(kernel, seq_n, head_n), out_shape=(jax.S...  56.4 us

profile of v2, /device:TPU:1, one launch (start us, length us, event | category | flops | bytes accessed | tf_op | source)
XLA Modules:
  0.0 58.1 jit_solution(7104999477737416958)
XLA Ops:
  0.6 56.4 %table_attention.1 = (bf16[2,8,32,128]{3,2,1,0:T(8,128)(2,1)S(1)}, bf16[256,1024]{1,0:T(8,128)(2,1)S(1)}, bf16[256,1024]{1,0:T(8,128)(2,1)S(1)}) custom-call(s32[2]{0:T(128)} %header_hbm.1, s32[2,3]{1,0:T(2,128)} %related_hbm.1, bf16[256,1024]{1,0:T(8,128)(2,1)} %q_hbm.1, bf16[256,1024]{1,0:T(8,128)(2,1)} %u_hbm.1, bf16[32,1024]{1,0:T(8,128)(2,1)} %k_hbm.1, ...), custom_call_target="tpu_custom_call" | custom-call | tf_op jit(solution)/shard_map/table_attention/pallas_call | solution.py:455
  57.0 1.1 %write_results.1 = (bf16[256,1024]{1,0:T(8,128)(2,1)}, bf16[256,1024]{1,0:T(8,128)(2,1)}, f32[32,1024]{1,0:T(8,128)}, f32[32,1024]{1,0:T(8,128)}) custom-call(bf16[2,8,32,128]{3,2,1,0:T(8,128)(2,1)S(1)} %get-tuple-element.7.home, bf16[256,1024]{1,0:T(8,128)(2,1)S(1)} %get-tuple-element.8.att_v, bf16[256,1024]{1,0:T(8,128)(2,1)S(1)} %get-tuple-element.9.dq_v), custom_call_target="tpu_custom_call" | custom-call | tf_op jit(solution)/shard_map/write_results/pallas_call | solution.py:501

commit v3 on v2

--- a/solution.py
+++ b/solution.py
@@ -57,15 +57,20 @@
     rbuf,
     gbuf,
     backb,
+    backn,
     widen,
     a_send,
     a_recv,
+    n_send,
+    n_recv,
     f_send,
     f_recv,
     r_send,
     r_recv,
     b_send,
     b_recv,
+    c_send,
+    c_recv,
     ld_sem,
     header,
     related,
@@ -84,8 +89,10 @@
         pl.semaphore_signal(
             barrier, inc=1, device_id={"head": lax.rem(me + off, head_n)}
         )
-    pl.semaphore_signal(barrier, inc=1, device_id={"seq": nxt})
-    pl.semaphore_signal(barrier, inc=1, device_id={"seq": prv})
+    for off in range(head_n):
+        peer = lax.rem(me + off, head_n)
+        for row in (nxt, prv):
+            pl.semaphore_signal(barrier, inc=1, device_id={"seq": row, "head": peer})
 
     def load(n):
         t, j = n // GROUP, n % GROUP
@@ -96,29 +103,34 @@
             pltpu.make_async_copy(u_hbm.at[rows, cols], u_r.at[at, :], ld_sem.at[1, n]),
         )
 
-    pl.semaphore_wait(barrier, head_n + 1)
-
-    def mine(x, h):
-        return pl.ds(own + h * part, part)
+    pl.semaphore_wait(barrier, 3 * head_n - 1)
 
     sends = []
+    ahead = own - 2 * BLOCK
+    order = sorted(range(head_n), key=lambda off: -min(off, head_n - off))
     for x, src in ((0, k_hbm), (1, v_hbm)):
         pltpu.make_async_copy(
             src.at[:, pl.ds(me * D, D)],
             win.at[x, pl.ds(own + me * part, part), :],
             a_recv.at[x, me],
         ).start()
-        for off in range(1, head_n):
-            peer = lax.rem(me + off, head_n)
-            copy = pltpu.make_async_remote_copy(
-                src_ref=src.at[:, pl.ds(peer * D, D)],
-                dst_ref=win.at[x, pl.ds(own + me * part, part), :],
-                send_sem=a_send.at[x, off],
-                recv_sem=a_recv.at[x, me],
-                device_id={"head": peer},
-            )
-            copy.start()
-            sends.append(copy)
+        for row, base, done, sent in (
+            (nxt, ahead, n_recv, n_send),
+            (seq, own, a_recv, a_send),
+        ):
+            for off in order:
+                if row is seq and off == 0:
+                    continue
+                peer = lax.rem(me + off, head_n)
+                copy = pltpu.make_async_remote_copy(
+                    src_ref=src.at[:, pl.ds(peer * D, D)],
+                    dst_ref=win.at[x, pl.ds(base + me * part, part), :],
+                    send_sem=sent.at[x, off],
+                    recv_sem=done.at[x, me],
+                    device_id={"seq": row, "head": peer},
+                )
+                copy.start()
+                sends.append(copy)
 
     tables = (
         pltpu.make_async_copy(header_hbm, header, table_sem.at[0]),
@@ -130,41 +142,34 @@
         for copy in load(n):
             copy.start()
 
-    def gathered(x, hi):
+    def gathered(x, hi, base, done):
         for h in range(half * hi, half * hi + half):
-            ref = win.at[x, pl.ds(own + h * part, part), :]
-            pltpu.make_async_copy(ref, ref, a_recv.at[x, h]).wait()
+            ref = win.at[x, pl.ds(base + h * part, part), :]
+            pltpu.make_async_copy(ref, ref, done.at[x, h]).wait()
+
+    def own_rows(x):
+        for hi in (1, 0):
+            gathered(x, hi, own, a_recv)
 
     def forward(x, k, hi):
         at = (NPOS - 2 - 2 * k + hi) * BLOCK
         return pltpu.make_async_remote_copy(
             src_ref=win.at[x, pl.ds(at, BLOCK), :],
             dst_ref=win.at[x, pl.ds(at - 2 * BLOCK, BLOCK), :],
-            send_sem=f_send.at[x, k, hi],
-            recv_sem=f_recv.at[x, k, hi],
+            send_sem=f_send.at[x, k - 1, hi],
+            recv_sem=f_recv.at[x, k - 1, hi],
             device_id={"seq": nxt},
         )
 
-    def pass_on(x, k, hi):
-        if k == REACH - 1 and hi == 0:
-            return
-        copy = forward(x, k, hi)
-        copy.start()
-        sends.append(copy)
-
-    def arrive(x, k, hi):
-        forward(x, k - 1, hi).wait_recv()
-
-    def relay(x, k):
-        for hi in (1, 0):
-            if k == REACH and hi == 0:
-                continue
-            if k == 0:
-                gathered(x, hi)
-            else:
-                arrive(x, k, hi)
-            if k < REACH:
-                pass_on(x, k, hi)
+    def relay(x, k, hi):
+        if k == 1:
+            gathered(x, hi, ahead, n_recv)
+        else:
+            forward(x, k - 1, hi).wait_recv()
+        if k < REACH - 1 or (k == REACH - 1 and hi == 1):
+            copy = forward(x, k, hi)
+            copy.start()
+            sends.append(copy)
 
     def pieces(k):
         if k == 0:
@@ -177,8 +182,10 @@
     def cols_of(n):
         return pl.ds(pl.multiple_of(n * QT, QT), QT)
 
-    def scores(k):
+    def scores(k, which=(0, 1)):
         for t, row, blocks in pieces(k):
+            if t not in which:
+                continue
             keys = win.at[0, pl.ds((row + t) * BLOCK, blocks * BLOCK), :]
             bias = [counts[t][SPAN - 1 - row - b] for b in range(blocks)]
 
@@ -300,15 +307,27 @@
             if k < REACH - 1 or (k == REACH - 1 and hi == 1):
                 backward(x, k + 1, hi).wait_recv()
                 total = total + rbuf[x, k, hi].astype(F32)
-            if k > 0:
-                sbuf[x, k - 1, hi] = total.astype(BF16)
+            sbuf[x, k - 1, hi] = total.astype(BF16)
+            if k > 1:
                 copy = backward(x, k, hi)
                 copy.start()
                 sends.append(copy)
-            else:
-                gbuf[x, pl.ds(hi * BLOCK, BLOCK), :] = total.astype(BF16)
-
-    def return_home(x):
+                continue
+            for h in range(half * hi, half * hi + half):
+                at = h * part - hi * BLOCK
+                copy = pltpu.make_async_remote_copy(
+                    src_ref=sbuf.at[x, 0, hi, pl.ds(at, part), :],
+                    dst_ref=backn.at[x, me],
+                    send_sem=c_send.at[x, h],
+                    recv_sem=c_recv.at[x, me],
+                    device_id={"seq": prv, "head": h},
+                )
+                copy.start()
+                sends.append(copy)
+
+    def own_home(x):
+        for hi in range(2):
+            gbuf[x, pl.ds(hi * BLOCK, BLOCK), :] = widen[x, 0, hi].astype(BF16)
         pltpu.make_async_copy(
             gbuf.at[x, pl.ds(me * part, part), :],
             backb.at[x, me],
@@ -327,18 +346,19 @@
             sends.append(copy)
 
     def write_home(x):
-        for h in range(head_n):
-            ref = backb.at[x, h]
-            pltpu.make_async_copy(ref, ref, b_recv.at[x, h]).wait()
-        home[x] = backb[x]
+        for n, (buf, done) in enumerate(((backb, b_recv), (backn, c_recv))):
+            for h in range(head_n):
+                ref = buf.at[x, h]
+                pltpu.make_async_copy(ref, ref, done.at[x, h]).wait()
+            home[n, x] = buf[x]
 
     def transposes(x):
         for p in range(NPOS):
             at = pl.ds(p * BLOCK, BLOCK)
             tr[x, :, at] = win[x, at, :].T
 
-    def row_output(x, left, stage, factor):
-        for t in range(2):
+    def row_output(x, left, stage, factor, which=(0, 1)):
+        for t in which:
 
             def body(n, carry, t=t):
                 cols = pl.ds(pl.multiple_of(n * 2 * D, 2 * D), 2 * D)
@@ -351,7 +371,8 @@
                 return carry
 
             lax.fori_loop(0, GROUP // 2, body, 0)
-    relay(0, 0)
+    relay(0, 1, 1)
+    relay(0, 1, 0)
     for copy in tables:
         copy.wait()
     counts = []
@@ -373,56 +394,68 @@
     for n in range(2 * GROUP):
         for copy in load(n):
             copy.wait()
-    relay(1, 0)
+    own_rows(0)
+    relay(1, 1, 1)
     scores(0)
-    dprobs(0)
-    for k in range(1, REACH):
-        relay(0, k)
-        scores(k)
-        relay(1, k)
-        dprobs(k)
-    relay(0, REACH)
+    relay(0, 2, 1)
+    relay(0, 2, 0)
+    relay(1, 1, 0)
+    scores(1, (0,))
+    relay(1, 2, 1)
+    scores(1, (1,))
+    relay(0, 3, 1)
+    relay(0, 3, 0)
+    relay(1, 2, 0)
+    scores(2)
+    relay(1, 3, 1)
+    scores(3)
+    relay(0, REACH, 1)
     scores(REACH)
     finish_sums()
     settle(REACH, grads=False)
     local_terms(1, REACH)
     reduce_send(1, REACH)
-    relay(1, REACH)
+    own_rows(1)
+    dprobs(0)
+    dprobs(1)
+    settle(3, grads=False)
+    local_terms(1, 3)
+    dprobs(2)
+    relay(1, 3, 0)
+    dprobs(3)
+    relay(1, REACH, 1)
     dprobs(REACH)
     finish_delta()
     settle(REACH, probs=False)
     local_terms(0, REACH)
     reduce_send(0, REACH)
-    settle(3)
-    local_terms(1, 3)
+    reduce_send(1, 3)
+    settle(3, probs=False)
     local_terms(0, 3)
     settle(2)
-    reduce_send(1, 3)
+    local_terms(1, 2)
     reduce_send(0, 3)
-    local_terms(1, 2)
+    reduce_send(1, 2)
     local_terms(0, 2)
     settle(1)
     local_terms(1, 1)
-    reduce_send(1, 2)
     reduce_send(0, 2)
+    reduce_send(1, 1)
     local_terms(0, 1)
     settle(0)
+    reduce_send(0, 1)
     local_terms(1, 0)
+    own_home(1)
     local_terms(0, 0)
-    reduce_send(1, 1)
-    reduce_send(0, 1)
+    own_home(0)
     transposes(1)
     row_output(1, plow, att_v, 1.0)
     transposes(0)
-    reduce_send(1, 0)
-    return_home(1)
-    reduce_send(0, 0)
-    return_home(0)
     row_output(0, dlow, dq_v, SCALE)
+    for copy in sends:
+        copy.wait_send()
     write_home(1)
     write_home(0)
-    for copy in sends:
-        copy.wait_send()
 
 
 def emit(home, att_v, dq_v, att, dq, dk, dv, wide, sems):
@@ -433,8 +466,10 @@
     for copy in copies:
         copy.start()
     for x, target in ((0, dk), (1, dv)):
-        for h in range(home.shape[1]):
-            wide[x, :, h * D : (h + 1) * D] = home[x, h].astype(F32)
+        for h in range(home.shape[2]):
+            wide[x, :, h * D : (h + 1) * D] = home[0, x, h].astype(F32) + home[
+                1, x, h
+            ].astype(F32)
         copy = pltpu.make_async_copy(wide.at[x], target, sems.at[x])
         copy.start()
         copies.append(copy)
@@ -455,7 +490,7 @@
     home, att, dq = pl.pallas_call(
         functools.partial(kernel, seq_n, head_n),
         out_shape=(
-            jax.ShapeDtypeStruct((2, head_n, part, D), BF16),
+            jax.ShapeDtypeStruct((2, 2, head_n, part, D), BF16),
             jax.ShapeDtypeStruct(queries.shape, BF16),
             jax.ShapeDtypeStruct(queries.shape, BF16),
         ),
@@ -477,13 +512,18 @@
             pltpu.VMEM((2, REACH, 2, BLOCK, D), BF16),
             pltpu.VMEM((2, 2 * BLOCK, D), BF16),
             pltpu.VMEM((2, head_n, part, D), BF16),
+            pltpu.VMEM((2, head_n, part, D), BF16),
             pltpu.VMEM((2, REACH + 1, 2, BLOCK, D), F32),
+            dma((2, head_n)),
+            dma((2, head_n)),
             dma((2, head_n)),
             dma((2, head_n)),
             dma((2, REACH, 2)),
             dma((2, REACH, 2)),
             dma((2, REACH, 2)),
             dma((2, REACH, 2)),
+            dma((2, head_n)),
+            dma((2, head_n)),
             dma((2, head_n)),
             dma((2, head_n)),
             dma((2, 2 * GROUP)),

time: 58.3 us -> 58.6 us (level)
  no operation moved by 1% of the time
where the time goes in v3:
time: 58.6 us; the launch traced here: 58.5 us
  Pallas kernels  57.8 us (99%)
  between operations  0.64 us (1%)
    pallas_call x1, Pallas kernels, per_device(): pl.pallas_call(functools.partial(kernel, seq_n, head_n), out_shape=(jax.S...  56.7 us

profile of v3, /device:TPU:1, one launch (start us, length us, event | category | flops | bytes accessed | tf_op | source)
XLA Modules:
  0.0 58.5 jit_solution(12806420358377362406)
XLA Ops:
  0.6 56.7 %table_attention.1 = (bf16[2,2,8,32,128]{4,3,2,1,0:T(8,128)(2,1)S(1)}, bf16[256,1024]{1,0:T(8,128)(2,1)S(1)}, bf16[256,1024]{1,0:T(8,128)(2,1)S(1)}) custom-call(s32[2]{0:T(128)} %header_hbm.1, s32[2,3]{1,0:T(2,128)} %related_hbm.1, bf16[256,1024]{1,0:T(8,128)(2,1)} %q_hbm.1, bf16[256,1024]{1,0:T(8,128)(2,1)} %u_hbm.1, bf16[32,1024]{1,0:T(8,128)(2,1)} %k_hbm.1, ...), custom_call_target="tpu_custom_call" | custom-call | tf_op jit(solution)/shard_map/table_attention/pallas_call | solution.py:490
  57.4 1.1 %write_results.1 = (bf16[256,1024]{1,0:T(8,128)(2,1)}, bf16[256,1024]{1,0:T(8,128)(2,1)}, f32[32,1024]{1,0:T(8,128)}, f32[32,1024]{1,0:T(8,128)}) custom-call(bf16[2,2,8,32,128]{4,3,2,1,0:T(8,128)(2,1)S(1)} %get-tuple-element.7.home, bf16[256,1024]{1,0:T(8,128)(2,1)S(1)} %get-tuple-element.8.att_v, bf16[256,1024]{1,0:T(8,128)(2,1)S(1)} %get-tuple-element.9.dq_v), custom_call_target="tpu_custom_call" | custom-call | tf_op jit(solution)/shard_map/write_results/pallas_call | solution.py:541

commit v4 on v3

--- a/solution.py
+++ b/solution.py
@@ -16,6 +16,8 @@
 NPOS = 9
 REACH = 4
 QT = 512
+CHUNK = 64
+ORDER = (2, 3, 0, 1)
 BIG = 1e30
 SCALE = 1.0 / math.sqrt(D)
 C2 = SCALE * math.log2(math.e)
@@ -81,7 +83,7 @@
     nxt = lax.rem(seq + 1, seq_n)
     prv = lax.rem(seq + seq_n - 1, seq_n)
     part = (2 * BLOCK) // head_n
-    half = head_n // 2
+    quarter = head_n // 4
     own = (NPOS - 2) * BLOCK
 
     barrier = pltpu.get_barrier_semaphore()
@@ -142,34 +144,35 @@
         for copy in load(n):
             copy.start()
 
-    def gathered(x, hi, base, done):
-        for h in range(half * hi, half * hi + half):
+    def gathered(x, p, base, done):
+        for h in range(p * quarter, p * quarter + quarter):
             ref = win.at[x, pl.ds(base + h * part, part), :]
             pltpu.make_async_copy(ref, ref, done.at[x, h]).wait()
 
     def own_rows(x):
-        for hi in (1, 0):
-            gathered(x, hi, own, a_recv)
-
-    def forward(x, k, hi):
-        at = (NPOS - 2 - 2 * k + hi) * BLOCK
+        for p in ORDER:
+            gathered(x, p, own, a_recv)
+
+    def forward(x, k, p):
+        at = (NPOS - 2 - 2 * k) * BLOCK + p * CHUNK
         return pltpu.make_async_remote_copy(
-            src_ref=win.at[x, pl.ds(at, BLOCK), :],
-            dst_ref=win.at[x, pl.ds(at - 2 * BLOCK, BLOCK), :],
-            send_sem=f_send.at[x, k - 1, hi],
-            recv_sem=f_recv.at[x, k - 1, hi],
+            src_ref=win.at[x, pl.ds(at, CHUNK), :],
+            dst_ref=win.at[x, pl.ds(at - 2 * BLOCK, CHUNK), :],
+            send_sem=f_send.at[x, k - 1, p],
+            recv_sem=f_recv.at[x, k - 1, p],
             device_id={"seq": nxt},
         )
 
-    def relay(x, k, hi):
-        if k == 1:
-            gathered(x, hi, ahead, n_recv)
-        else:
-            forward(x, k - 1, hi).wait_recv()
-        if k < REACH - 1 or (k == REACH - 1 and hi == 1):
-            copy = forward(x, k, hi)
-            copy.start()
-            sends.append(copy)
+    def relay(x, k):
+        for p in ORDER if k < REACH else ORDER[:2]:
+            if k == 1:
+                gathered(x, p, ahead, n_recv)
+            else:
+                forward(x, k - 1, p).wait_recv()
+            if k < REACH - 1 or (k == REACH - 1 and p >= 2):
+                copy = forward(x, k, p)
+                copy.start()
+                sends.append(copy)
 
     def pieces(k):
         if k == 0:
@@ -286,37 +289,36 @@
                 found[hi] = found[hi] + term if hi in found else term
         return {hi: term * factor for hi, term in found.items()}
 
-    def backward(x, k, hi):
+    def backward(x, k, p):
+        rows = pl.ds(p * CHUNK, CHUNK)
         return pltpu.make_async_remote_copy(
-            src_ref=sbuf.at[x, k - 1, hi],
-            dst_ref=rbuf.at[x, k - 1, hi],
-            send_sem=r_send.at[x, k - 1, hi],
-            recv_sem=r_recv.at[x, k - 1, hi],
+            src_ref=sbuf.at[x, k - 1, rows, :],
+            dst_ref=rbuf.at[x, k - 1, rows, :],
+            send_sem=r_send.at[x, k - 1, p],
+            recv_sem=r_recv.at[x, k - 1, p],
             device_id={"seq": prv},
         )
 
     def local_terms(x, k):
         for hi, term in terms(x, k).items():
-            widen[x, k, hi] = term
+            widen[x, k, pl.ds(hi * BLOCK, BLOCK), :] = term
 
     def reduce_send(x, k):
-        for hi in (1, 0):
-            if k == REACH and hi == 0:
-                continue
-            total = widen[x, k, hi]
-            if k < REACH - 1 or (k == REACH - 1 and hi == 1):
-                backward(x, k + 1, hi).wait_recv()
-                total = total + rbuf[x, k, hi].astype(F32)
-            sbuf[x, k - 1, hi] = total.astype(BF16)
+        for p in ORDER if k < REACH else ORDER[:2]:
+            rows = pl.ds(p * CHUNK, CHUNK)
+            total = widen[x, k, rows, :]
+            if k < REACH - 1 or (k == REACH - 1 and p >= 2):
+                backward(x, k + 1, p).wait_recv()
+                total = total + rbuf[x, k, rows, :].astype(F32)
+            sbuf[x, k - 1, rows, :] = total.astype(BF16)
             if k > 1:
-                copy = backward(x, k, hi)
+                copy = backward(x, k, p)
                 copy.start()
                 sends.append(copy)
                 continue
-            for h in range(half * hi, half * hi + half):
-                at = h * part - hi * BLOCK
+            for h in range(p * quarter, p * quarter + quarter):
                 copy = pltpu.make_async_remote_copy(
-                    src_ref=sbuf.at[x, 0, hi, pl.ds(at, part), :],
+                    src_ref=sbuf.at[x, 0, pl.ds(h * part, part), :],
                     dst_ref=backn.at[x, me],
                     send_sem=c_send.at[x, h],
                     recv_sem=c_recv.at[x, me],
@@ -326,8 +328,7 @@
                 sends.append(copy)
 
     def own_home(x):
-        for hi in range(2):
-            gbuf[x, pl.ds(hi * BLOCK, BLOCK), :] = widen[x, 0, hi].astype(BF16)
+        gbuf[x] = widen[x, 0].astype(BF16)
         pltpu.make_async_copy(
             gbuf.at[x, pl.ds(me * part, part), :],
             backb.at[x, me],
@@ -371,8 +372,7 @@
                 return carry
 
             lax.fori_loop(0, GROUP // 2, body, 0)
-    relay(0, 1, 1)
-    relay(0, 1, 0)
+    relay(0, 1)
     for copy in tables:
         copy.wait()
     counts = []
@@ -395,42 +395,35 @@
         for copy in load(n):
             copy.wait()
     own_rows(0)
-    relay(1, 1, 1)
     scores(0)
-    relay(0, 2, 1)
-    relay(0, 2, 0)
-    relay(1, 1, 0)
-    scores(1, (0,))
-    relay(1, 2, 1)
-    scores(1, (1,))
-    relay(0, 3, 1)
-    relay(0, 3, 0)
-    relay(1, 2, 0)
+    relay(1, 1)
+    relay(0, 2)
+    scores(1)
+    own_rows(1)
+    dprobs(0)
+    relay(1, 2)
+    relay(0, 3)
     scores(2)
-    relay(1, 3, 1)
+    dprobs(1)
+    relay(1, 3)
     scores(3)
-    relay(0, REACH, 1)
+    relay(0, REACH)
     scores(REACH)
     finish_sums()
     settle(REACH, grads=False)
     local_terms(1, REACH)
     reduce_send(1, REACH)
-    own_rows(1)
-    dprobs(0)
-    dprobs(1)
-    settle(3, grads=False)
-    local_terms(1, 3)
     dprobs(2)
-    relay(1, 3, 0)
     dprobs(3)
-    relay(1, REACH, 1)
+    relay(1, REACH)
     dprobs(REACH)
     finish_delta()
     settle(REACH, probs=False)
     local_terms(0, REACH)
     reduce_send(0, REACH)
+    settle(3)
+    local_terms(1, 3)
     reduce_send(1, 3)
-    settle(3, probs=False)
     local_terms(0, 3)
     settle(2)
     local_terms(1, 2)
@@ -443,11 +436,11 @@
     reduce_send(1, 1)
     local_terms(0, 1)
     settle(0)
-    reduce_send(0, 1)
     local_terms(1, 0)
     own_home(1)
     local_terms(0, 0)
     own_home(0)
+    reduce_send(0, 1)
     transposes(1)
     row_output(1, plow, att_v, 1.0)
     transposes(0)
@@ -508,20 +501,20 @@
             pltpu.VMEM((2, 8, QROWS), F32),
             pltpu.VMEM((2, 8, QROWS), F32),
             pltpu.VMEM((2, 8, QROWS), F32),
-            pltpu.VMEM((2, REACH, 2, BLOCK, D), BF16),
-            pltpu.VMEM((2, REACH, 2, BLOCK, D), BF16),
+            pltpu.VMEM((2, REACH, 2 * BLOCK, D), BF16),
+            pltpu.VMEM((2, REACH, 2 * BLOCK, D), BF16),
             pltpu.VMEM((2, 2 * BLOCK, D), BF16),
             pltpu.VMEM((2, head_n, part, D), BF16),
             pltpu.VMEM((2, head_n, part, D), BF16),
-            pltpu.VMEM((2, REACH + 1, 2, BLOCK, D), F32),
-            dma((2, head_n)),
-            dma((2, head_n)),
-            dma((2, head_n)),
-            dma((2, head_n)),
-            dma((2, REACH, 2)),
-            dma((2, REACH, 2)),
-            dma((2, REACH, 2)),
-            dma((2, REACH, 2)),
+            pltpu.VMEM((2, REACH + 1, 2 * BLOCK, D), F32),
+            dma((2, head_n)),
+            dma((2, head_n)),
+            dma((2, head_n)),
+            dma((2, head_n)),
+            dma((2, REACH, 4)),
+            dma((2, REACH, 4)),
+            dma((2, REACH, 4)),
+            dma((2, REACH, 4)),
             dma((2, head_n)),
             dma((2, head_n)),
             dma((2, head_n)),

time: 58.6 us -> 56.6 us (0.966)
  Pallas kernels: 57.8 us -> 55.8 us
    pallas_call x1, Pallas kernels: 56.7 us -> 54.7 us  [per_device(): pl.pallas_call(functools.partial(kernel, seq_n, head_n), out_shape=(jax.S...]
where the time goes in v4:
time: 56.6 us; the launch traced here: 56.4 us
  Pallas kernels  55.8 us (99%)
  between operations  0.64 us (1%)
    pallas_call x1, Pallas kernels, per_device(): pl.pallas_call(functools.partial(kernel, seq_n, head_n), out_shape=(jax.S...  54.7 us

profile of v4, /device:TPU:1, one launch (start us, length us, event | category | flops | bytes accessed | tf_op | source)
XLA Modules:
  0.0 56.4 jit_solution(14011973626286241442)
XLA Ops:
  0.6 54.7 %table_attention.1 = (bf16[2,2,8,32,128]{4,3,2,1,0:T(8,128)(2,1)S(1)}, bf16[256,1024]{1,0:T(8,128)(2,1)S(1)}, bf16[256,1024]{1,0:T(8,128)(2,1)S(1)}) custom-call(s32[2]{0:T(128)} %header_hbm.1, s32[2,3]{1,0:T(2,128)} %related_hbm.1, bf16[256,1024]{1,0:T(8,128)(2,1)} %q_hbm.1, bf16[256,1024]{1,0:T(8,128)(2,1)} %u_hbm.1, bf16[32,1024]{1,0:T(8,128)(2,1)} %k_hbm.1, ...), custom_call_target="tpu_custom_call" | custom-call | tf_op jit(solution)/shard_map/table_attention/pallas_call | solution.py:483
  55.3 1.1 %write_results.1 = (bf16[256,1024]{1,0:T(8,128)(2,1)}, bf16[256,1024]{1,0:T(8,128)(2,1)}, f32[32,1024]{1,0:T(8,128)}, f32[32,1024]{1,0:T(8,128)}) custom-call(bf16[2,2,8,32,128]{4,3,2,1,0:T(8,128)(2,1)S(1)} %get-tuple-element.7.home, bf16[256,1024]{1,0:T(8,128)(2,1)S(1)} %get-tuple-element.8.att_v, bf16[256,1024]{1,0:T(8,128)(2,1)S(1)} %get-tuple-element.9.dq_v), custom_call_target="tpu_custom_call" | custom-call | tf_op jit(solution)/shard_map/write_results/pallas_call | solution.py:534

commit v5 on v4

--- a/solution.py
+++ b/solution.py
@@ -18,6 +18,7 @@
 QT = 512
 CHUNK = 64
 ORDER = (2, 3, 0, 1)
+BACK = (0, 1, 2, 3)
 BIG = 1e30
 SCALE = 1.0 / math.sqrt(D)
 C2 = SCALE * math.log2(math.e)
@@ -219,7 +220,7 @@
                 mhist[t, k : k + 1, cols] = top
                 return carry
 
-            lax.fori_loop(0, QROWS // QT, body, 0)
+            lax.fori_loop(0, QROWS // QT, body, 0, unroll=True)
 
     def finish_sums():
         for t in range(2):
@@ -244,7 +245,7 @@
                 )
                 return carry
 
-            lax.fori_loop(0, QROWS // QT, body, 0)
+            lax.fori_loop(0, QROWS // QT, body, 0, unroll=True)
 
     def finish_delta():
         for t in range(2):
@@ -269,7 +270,7 @@
                     ).astype(BF16)
                 return carry
 
-            lax.fori_loop(0, QROWS // QT, body, 0)
+            lax.fori_loop(0, QROWS // QT, body, 0, unroll=True)
 
     def terms(x, k):
         left, right, factor = (
@@ -304,7 +305,7 @@
             widen[x, k, pl.ds(hi * BLOCK, BLOCK), :] = term
 
     def reduce_send(x, k):
-        for p in ORDER if k < REACH else ORDER[:2]:
+        for p in BACK if k < REACH else BACK[2:]:
             rows = pl.ds(p * CHUNK, CHUNK)
             total = widen[x, k, rows, :]
             if k < REACH - 1 or (k == REACH - 1 and p >= 2):

time: 56.6 us -> 52.4 us (0.926)
  Pallas kernels: 55.8 us -> 51.6 us
    pallas_call x1, Pallas kernels: 54.7 us -> 50.5 us  [per_device(): pl.pallas_call(functools.partial(kernel, seq_n, head_n), out_shape=(jax.S...]
where the time goes in v5:
time: 52.4 us; the launch traced here: 52.2 us
  Pallas kernels  51.6 us (98%)
  between operations  0.64 us (1%)
    pallas_call x1, Pallas kernels, per_device(): pl.pallas_call(functools.partial(kernel, seq_n, head_n), out_shape=(jax.S...  50.5 us
    pallas_call x1, Pallas kernels, per_device(): pl.pallas_call(emit, out_shape=(jax.ShapeDtypeStruct(queries.shape, BF16)...  1.08 us

profile of v5, /device:TPU:1, one launch (start us, length us, event | category | flops | bytes accessed | tf_op | source)
XLA Modules:
  0.0 52.2 jit_solution(5174848735897210920)
XLA Ops:
  0.6 50.5 %table_attention.1 = (bf16[2,2,8,32,128]{4,3,2,1,0:T(8,128)(2,1)S(1)}, bf16[256,1024]{1,0:T(8,128)(2,1)S(1)}, bf16[256,1024]{1,0:T(8,128)(2,1)S(1)}) custom-call(s32[2]{0:T(128)} %header_hbm.1, s32[2,3]{1,0:T(2,128)} %related_hbm.1, bf16[256,1024]{1,0:T(8,128)(2,1)} %q_hbm.1, bf16[256,1024]{1,0:T(8,128)(2,1)} %u_hbm.1, bf16[32,1024]{1,0:T(8,128)(2,1)} %k_hbm.1, ...), custom_call_target="tpu_custom_call" | custom-call | tf_op jit(solution)/shard_map/table_attention/pallas_call | solution.py:484
  51.1 1.1 %write_results.1 = (bf16[256,1024]{1,0:T(8,128)(2,1)}, bf16[256,1024]{1,0:T(8,128)(2,1)}, f32[32,1024]{1,0:T(8,128)}, f32[32,1024]{1,0:T(8,128)}) custom-call(bf16[2,2,8,32,128]{4,3,2,1,0:T(8,128)(2,1)S(1)} %get-tuple-element.7.home, bf16[256,1024]{1,0:T(8,128)(2,1)S(1)} %get-tuple-element.8.att_v, bf16[256,1024]{1,0:T(8,128)(2,1)S(1)} %get-tuple-element.9.dq_v), custom_call_target="tpu_custom_call" | custom-call | tf_op jit(solution)/shard_map/write_results/pallas_call | solution.py:535

commit v6 on v5

--- a/solution.py
+++ b/solution.py
@@ -417,6 +417,8 @@
     dprobs(2)
     dprobs(3)
     relay(1, REACH)
+    early = sends[:]
+    sends.clear()
     dprobs(REACH)
     finish_delta()
     settle(REACH, probs=False)
@@ -433,6 +435,8 @@
     local_terms(0, 2)
     settle(1)
     local_terms(1, 1)
+    for copy in early:
+        copy.wait_send()
     reduce_send(0, 2)
     reduce_send(1, 1)
     local_terms(0, 1)

time: 52.4 us -> 52.3 us (level)
  no operation moved by 1% of the time
where the time goes in v6:
time: 52.3 us; the launch traced here: 52.2 us
  Pallas kernels  51.6 us (99%)
  between operations  0.64 us (1%)
    pallas_call x1, Pallas kernels, per_device(): pl.pallas_call(functools.partial(kernel, seq_n, head_n), out_shape=(jax.S...  50.5 us
    pallas_call x1, Pallas kernels, per_device(): pl.pallas_call(emit, out_shape=(jax.ShapeDtypeStruct(queries.shape, BF16)...  1.08 us

profile of v6, /device:TPU:1, one launch (start us, length us, event | category | flops | bytes accessed | tf_op | source)
XLA Modules:
  0.0 52.2 jit_solution(184852924357215812)
XLA Ops:
  0.6 50.5 %table_attention.1 = (bf16[2,2,8,32,128]{4,3,2,1,0:T(8,128)(2,1)S(1)}, bf16[256,1024]{1,0:T(8,128)(2,1)S(1)}, bf16[256,1024]{1,0:T(8,128)(2,1)S(1)}) custom-call(s32[2]{0:T(128)} %header_hbm.1, s32[2,3]{1,0:T(2,128)} %related_hbm.1, bf16[256,1024]{1,0:T(8,128)(2,1)} %q_hbm.1, bf16[256,1024]{1,0:T(8,128)(2,1)} %u_hbm.1, bf16[32,1024]{1,0:T(8,128)(2,1)} %k_hbm.1, ...), custom_call_target="tpu_custom_call" | custom-call | tf_op jit(solution)/shard_map/table_attention/pallas_call | solution.py:488
  51.1 1.1 %write_results.1 = (bf16[256,1024]{1,0:T(8,128)(2,1)}, bf16[256,1024]{1,0:T(8,128)(2,1)}, f32[32,1024]{1,0:T(8,128)}, f32[32,1024]{1,0:T(8,128)}) custom-call(bf16[2,2,8,32,128]{4,3,2,1,0:T(8,128)(2,1)S(1)} %get-tuple-element.7.home, bf16[256,1024]{1,0:T(8,128)(2,1)S(1)} %get-tuple-element.8.att_v, bf16[256,1024]{1,0:T(8,128)(2,1)S(1)} %get-tuple-element.9.dq_v), custom_call_target="tpu_custom_call" | custom-call | tf_op jit(solution)/shard_map/write_results/pallas_call | solution.py:539
